TPU v7x, 32 devices: a whole 2x2x4 slice. The times are simulated.
32 devices in a mesh: section: 4 (over y, core), dp: 8 (over z, x).
Axes of the slice: x: 2, y: 2, z: 4, core: 2. Of those that a mesh axis runs over, the one named last changes fastest.
Arguments:
- fresh_batches: bfloat16 [3, 512, 4096], P(None, 'dp'), may hold values from -6 to 6
- held_states: bfloat16 [4, 512, 4096], P('section', 'dp'), may hold values from -6 to 6
- section_weight: bfloat16 [4, 4096, 4096], P('section', None, 'dp'), may hold values from -0.09375 to 0.09375
- section_gain: float32 [4, 4096], P('section'), may hold values from 0.25 to 1.75
- final_gain: float32 [4096], replicated, may hold values from 0.3 to 3
- cached_pool: bfloat16 [512, 4096], P('dp'), may hold values from -0.09375 to 0.09375
- route: int32 [8, 64], P('dp'), may hold values from 0 to 63, each once within a row
- queries: bfloat16 [256, 4096], P(('section', 'dp')), may hold values from -0.09375 to 0.09375
- shortlist: int32 [256, 128], P(('section', 'dp')), may hold values from 0 to 63
- teacher: float32 [256, 128], P(('section', 'dp')), may hold values from -16 to 300, as said below
Outputs:
- held_out: bfloat16 [4, 512, 4096], P('section', 'dp')
- losses: float32 [256], P(('section', 'dp'))
- query_grad: float32 [256, 4096], P(('section', 'dp'))
- pool_grad: bfloat16 [512, 4096], P('dp')
Inputs may be any that keep to these rules, and one draw needn't show every extreme that they name: `teacher`: reranker scores; on some draws some rows have two entries above the rest.
All inputs are finite; a program needn't handle non-finite values.
Results may differ from a plain program's by a relative error of at most 0.0058.
Values may be sent and summed in bfloat16 or wider, within the bound.
No kernel may reach another device: no remote copies, remote signals or barrier semaphores. Data moves between devices by JAX's collectives and lax.ppermute only.
A program may use at most 64 MiB of HBM per device.

v0:
```python
import jax
import jax.numpy as jnp
from jax import lax
from jax.sharding import PartitionSpec as P

SEQ = 128
TICKS = 3


epsilon = 1e-06
logit_scale = 20.0


def from_behind(x, axis, by):
    length = lax.axis_size(axis)
    pairs = [(i, i + by) for i in range(length) if 0 <= i + by < length]
    return lax.ppermute(x, axis, pairs)


def from_root(value, axis, source):
    kept = jnp.where(lax.axis_index(axis) == source, value, 0).astype(value.dtype)
    return lax.psum(kept, axis)


def on_device(
    fresh_batches,
    held_states,
    section_weight,
    section_gain,
    final_gain,
    cached_pool,
    route,
    queries,
    shortlist,
    teacher,
):
    section_index = lax.axis_index("section")
    section_count = lax.axis_size("section")
    dp_index = lax.axis_index("dp")
    weight = section_weight[0]
    layer_gain = section_gain[0]
    tok_dev = held_states.shape[1]
    current = held_states[0]
    exit_list = []
    for tick_index in range(TICKS):
        widened = current.astype(jnp.float32)
        inv_rms = lax.rsqrt(jnp.mean(widened * widened, axis=-1, keepdims=True) + epsilon)
        normed = (widened * inv_rms * layer_gain).astype(jnp.bfloat16)
        columns = jnp.dot(
            lax.all_gather(normed, "dp", axis=0, tiled=True),
            weight,
            preferred_element_type=jnp.float32,
        ).astype(jnp.bfloat16)
        projected = lax.all_to_all(columns, "dp", split_axis=0, concat_axis=1, tiled=True)
        result_rows = (widened + jax.nn.silu(projected.astype(jnp.float32))).astype(jnp.bfloat16)
        scaled = result_rows[tok_dev - 1].astype(jnp.float32) * final_gain
        exit_list.append(
            (scaled * lax.rsqrt(jnp.sum(scaled * scaled) + epsilon)).astype(jnp.bfloat16)
        )
        shifted = from_behind(result_rows, "section", 1)
        current = jnp.where(section_index == 0, fresh_batches[tick_index], shifted)
    exit_rows = jnp.stack(exit_list)
    is_end = (dp_index + 1) * tok_dev % SEQ == 0
    head_rows = jnp.where(is_end, exit_rows, cached_pool[:TICKS])
    pool_rows = jnp.concatenate([head_rows, cached_pool[TICKS:]], axis=0)
    outbox = jnp.take(pool_rows, route[0], axis=0)
    received = lax.all_to_all(outbox, "dp", split_axis=0, concat_axis=0, tiled=True)
    received = from_root(received, "section", section_count - 1)
    pool_size = received.shape[0]
    all_scores = lax.dot_general(
        queries, received, (((1,), (1,)), ((), ())), preferred_element_type=jnp.float32
    )
    student = jnp.take_along_axis(all_scores, shortlist, axis=1) * logit_scale
    student_log = jax.nn.log_softmax(student, axis=-1)
    teacher_log = jax.nn.log_softmax(teacher, axis=-1)
    teacher_prob = jnp.exp(teacher_log)
    losses = jnp.sum(teacher_prob * (teacher_log - student_log), axis=-1)
    logit_grad = logit_scale * (jnp.exp(student_log) - teacher_prob)
    one_hot = (shortlist[..., None] == jnp.arange(pool_size, dtype=jnp.int32)).astype(jnp.float32)
    pool_logit_grad = jnp.einsum("ij,ijr->ir", logit_grad, one_hot, precision=lax.Precision.HIGHEST)
    received_wide = received.astype(jnp.float32)
    query_grad = jnp.dot(pool_logit_grad, received_wide, precision=lax.Precision.HIGHEST)
    grad_terms = jnp.dot(
        pool_logit_grad.T, queries.astype(jnp.float32), precision=lax.Precision.HIGHEST
    )
    grad_whole = lax.psum(grad_terms, "section").astype(jnp.bfloat16)
    returned = lax.all_to_all(grad_whole, "dp", split_axis=0, concat_axis=0, tiled=True)
    pool_grad = jnp.zeros(returned.shape, jnp.bfloat16).at[route[0]].set(returned)
    return (current[None], losses, query_grad, pool_grad)


def solution(mesh):
    return jax.shard_map(
        on_device,
        mesh=mesh,
        in_specs=(
            P(None, "dp", None),
            P("section", "dp", None),
            P("section", None, "dp"),
            P("section", None),
            P(),
            P("dp", None),
            P("dp", None),
            P(("section", "dp"), None),
            P(("section", "dp"), None),
            P(("section", "dp"), None),
        ),
        out_specs=(
            P("section", "dp", None),
            P(("section", "dp")),
            P(("section", "dp"), None),
            P("dp", None),
        ),
        check_vma=False,
    )
```

profile of v0, /device:TPU:0, one launch (start us, length us, event | category | flops | bytes accessed | tf_op | source)
XLA Modules:
  0.0 448.5 jit_solution(9558564981494179745)
XLA Ops:
  8.5 2.0 fusion.25
  10.6 75.7 %all-gather.4.cloned.1.call-done = bf16[512,4096]{1,0:T(8,128)(2,1)} async-done(((bf16[64,4096]{1,0:T(8,128)(2,1)}), bf16[512,4096]{1,0:T(8,128)(2,1)}) %all-gather.4.cloned.1.call-update) | async-done | bytes 4194320 | tf_op jit(solution)/shard_map/all_gather | solution.py:50
  86.2 5.8 %fusion.6 = bf16[512,512]{1,0:T(8,128)(2,1)S(1)} fusion(bf16[512,4096]{1,0:T(8,128)(2,1)} %all-gather.4.cloned.1.call-done, bf16[1,4096,512]{2,1,0:T(8,128)(2,1)} %param.13), kind=kOutput, calls=%fused_computation.18 | convolution fusion | flops 2147745792 | bytes 8912896 | tf_op jit(solution)/shard_map/dot_general | solution.py:49
  92.1 17.6 %all_to_all.57 = bf16[8,64,512]{2,1,0:T(8,128)(2,1)S(1)} all-to-all(bf16[8,64,512]{2,1,0:T(8,128)(2,1)S(1)} %bitcast.96), channel_id=1, replica_groups=mesh['section'=4,'dp'=8] {'dp'}, dimensions={0} | all-to-all | bytes 1048576 | tf_op jit(solution)/shard_map/all_to_all | solution.py:54
  110.2 1.3 collective-permute-start
  111.5 1.5 collective-permute-done
  114.4 79.5 %all-gather.6.cloned.1.call-done = bf16[512,4096]{1,0:T(8,128)(2,1)} async-done(((bf16[64,4096]{1,0:T(8,128)(2,1)}), bf16[512,4096]{1,0:T(8,128)(2,1)}) %all-gather.6.cloned.1.call-update) | async-done | bytes 4194320 | tf_op jit(solution)/shard_map/all_gather | solution.py:50
  193.9 5.8 %fusion.9 = bf16[512,512]{1,0:T(8,128)(2,1)S(1)} fusion(bf16[512,4096]{1,0:T(8,128)(2,1)} %all-gather.6.cloned.1.call-done, bf16[1,4096,512]{2,1,0:T(8,128)(2,1)} %param.13), kind=kOutput, calls=%fused_computation.19 | convolution fusion | flops 2147745792 | bytes 8912896 | tf_op jit(solution)/shard_map/dot_general | solution.py:49
  199.7 17.4 %all_to_all.58 = bf16[8,64,512]{2,1,0:T(8,128)(2,1)S(1)} all-to-all(bf16[8,64,512]{2,1,0:T(8,128)(2,1)S(1)} %bitcast.97), channel_id=1, replica_groups=mesh['section'=4,'dp'=8] {'dp'}, dimensions={0} | all-to-all | bytes 1048576 | tf_op jit(solution)/shard_map/all_to_all | solution.py:54
  217.6 1.3 collective-permute-start.1
  218.9 1.5 collective-permute-done.1
  223.2 78.1 %all-gather.8.cloned.1.call-done = bf16[512,4096]{1,0:T(8,128)(2,1)} async-done(((bf16[64,4096]{1,0:T(8,128)(2,1)}), bf16[512,4096]{1,0:T(8,128)(2,1)}) %all-gather.8.cloned.1.call-update) | async-done | bytes 4194320 | tf_op jit(solution)/shard_map/all_gather | solution.py:50
  301.3 6.6 %fusion.12 = bf16[512,512]{1,0:T(8,128)(2,1)} fusion(bf16[512,4096]{1,0:T(8,128)(2,1)} %all-gather.8.cloned.1.call-done, bf16[1,4096,512]{2,1,0:T(8,128)(2,1)} %param.13), kind=kOutput, calls=%fused_computation.20 | convolution fusion | flops 2147745792 | bytes 8912896 | tf_op jit(solution)/shard_map/dot_general | solution.py:49
  307.9 3.6 all-to-all-start.2
  313.3 12.4 %all-to-all-done.2 = bf16[8,64,512]{2,1,0:T(8,128)(2,1)S(1)} async-done(((bf16[8,64,512]{2,1,0:T(8,128)(2,1)}), bf16[8,64,512]{2,1,0:T(8,128)(2,1)S(1)}, u32[]{:S(2)}, u32[]{:S(2)}) %all-to-all-start.2) | async-done | bytes 524320 | tf_op jit(solution)/shard_map/all_to_all | solution.py:54
  333.5 3.6 all-to-all-start.3
  337.3 14.3 %all-to-all-done.3 = bf16[8,8,4096]{2,1,0:T(8,128)(2,1)S(1)} async-done(((bf16[8,8,4096]{2,1,0:T(8,128)(2,1)}), bf16[8,8,4096]{2,1,0:T(8,128)(2,1)S(1)}, u32[]{:S(2)}, u32[]{:S(2)}) %all-to-all-start.3) | async-done | bytes 524320 | tf_op jit(solution)/shard_map/all_to_all | solution.py:67
  352.6 2.1 collective-permute-start.2
  354.7 30.7 %all-reduce.3.cloned.1.call-done = bf16[64,4096]{1,0:T(8,128)(2,1)} async-done(((bf16[64,4096]{1,0:T(8,128)(2,1)}), bf16[64,4096]{1,0:T(8,128)(2,1)}) %all-reduce.3.cloned.1.call-update) | async-done | bytes 524304 | tf_op jit(solution)/shard_map/psum | solution.py:22
  386.7 4.8 %gather_fusion.1 = f32[1024]{0:T(1024)S(1)} fusion(f32[8,64]{1,0:T(8,128)S(1)} %convolution_bitcast_fusion, s32[1024]{0:T(1024)S(1)} %fusion.34), kind=kCustom, calls=%fused_computation.1 | custom fusion | bytes 16384 | tf_op jit(solution)/shard_map/jit(take_along_axis)/gather | solution.py:73
  393.7 25.7 %all-reduce.4 = bf16[64,4096]{1,0:T(8,128)(2,1)} all-reduce(f32[64,4096]{1,0:T(8,128)S(1)} %fusion.39), channel_id=1, replica_groups=mesh['section'=4,'dp'=8] {'section'}, use_global_device_ids=true, to_apply=%region_10.12 | all-reduce | flops 262144 | bytes 1572864 | tf_op jit(solution)/shard_map/psum | solution.py:86
  419.4 5.4 %all-to-all-start.4 = ((bf16[8,8,4096]{2,1,0:T(8,128)(2,1)}), bf16[8,8,4096]{2,1,0:T(8,128)(2,1)S(1)}, u32[]{:S(2)}, u32[]{:S(2)}) async-start(bf16[8,8,4096]{2,1,0:T(8,128)(2,1)} %bitcast.77), calls=%async_computation.4 | async-start | bytes 1048576 | tf_op jit(solution)/shard_map/all_to_all | solution.py:87
  426.7 13.2 %all-to-all-done.4 = bf16[8,8,4096]{2,1,0:T(8,128)(2,1)S(1)} async-done(((bf16[8,8,4096]{2,1,0:T(8,128)(2,1)}), bf16[8,8,4096]{2,1,0:T(8,128)(2,1)S(1)}, u32[]{:S(2)}, u32[]{:S(2)}) %all-to-all-start.4) | async-done | bytes 524320 | tf_op jit(solution)/shard_map/all_to_all | solution.py:87
  439.9 2.1 scatter_custom_fusion
  (84 shorter events, 20.2 us)
Async XLA Ops:
  7.2 378.3 %copy-start = (bf16[8,4096]{1,0:T(8,128)(2,1)S(1)}, bf16[8,4096]{1,0:T(8,128)(2,1)}, u32[]{:S(2)}) copy-start(bf16[8,4096]{1,0:T(8,128)(2,1)} %param.18) | copy-start | bytes 196612
  7.2 79.1 %all-gather.4.cloned.1.call-start = ((), (), s32[]{:S(2)}) async-start(), calls=%async_computation.5 | async-start | bytes 4718592 | tf_op jit(solution)/shard_map/all_gather | solution.py:50
  10.5 183.3 %all-gather.6.cloned.1.call-start = ((), (), s32[]{:S(2)}) async-start(), calls=%async_computation.6 | async-start | bytes 4718592 | tf_op jit(solution)/shard_map/all_gather | solution.py:50
  92.0 17.8 %copy-start.1 = (bf16[1,64,4096]{2,1,0:T(8,128)(2,1)S(1)}, bf16[1,64,4096]{2,1,0:T(8,128)(2,1)}, u32[]{:S(2)}) copy-start(bf16[1,64,4096]{2,1,0:T(8,128)(2,1)} %param.12) | copy-start | bytes 1572868
  92.1 20.9 %copy-start.3 = (bf16[3,64,4096]{2,1,0:T(8,128)(2,1)S(1)}, bf16[3,64,4096]{2,1,0:T(8,128)(2,1)}, u32[]{:S(2)}) copy-start(bf16[3,64,4096]{2,1,0:T(8,128)(2,1)} %param.11) | copy-start | bytes 4718596
  92.1 21.2 %copy-start.7 = (f32[1,4096]{1,0:T(1,128)S(1)}, f32[1,4096]{1,0:T(1,128)}, u32[]{:S(2)}) copy-start(f32[1,4096]{1,0:T(1,128)} %param.14) | copy-start | bytes 49156
  110.2 1.4 copy-start.5
  110.2 2.8 collective-permute-start
  114.3 187.0 %all-gather.8.cloned.1.call-start = ((), (), s32[]{:S(2)}) async-start(), calls=%async_computation.7 | async-start | bytes 4718592 | tf_op jit(solution)/shard_map/all_gather | solution.py:50
  217.1 5.2 %copy-start.11 = (s32[1,64]{1,0:T(1,128)S(1)}, s32[1,64]{1,0:T(1,128)}, u32[]{:S(2)}) copy-start(s32[1,64]{1,0:T(1,128)} %param.17) | copy-start | bytes 772
  217.1 5.9 %copy-start.4 = (bf16[64,4096]{1,0:T(8,128)(2,1)S(1)}, bf16[64,4096]{1,0:T(8,128)(2,1)}, u32[]{:S(2)}) copy-start(bf16[64,4096]{1,0:T(8,128)(2,1)} %param.16) | copy-start | bytes 1572868
  217.6 5.3 %copy-start.6 = (bf16[64,4096]{1,0:T(8,128)(2,1)}, bf16[64,4096]{1,0:T(8,128)(2,1)S(1)}, u32[]{:S(2)}) copy-start(bf16[64,4096]{1,0:T(8,128)(2,1)S(1)} %fusion.18) | copy-start | bytes 1572868
  217.6 2.8 collective-permute-start.1
  307.9 20.0 %copy-start.9 = (f32[4096]{0:T(1024)S(1)}, f32[4096]{0:T(1024)}, u32[]{:S(2)}) copy-start(f32[4096]{0:T(1024)} %param.15) | copy-start | bytes 49156
  307.9 17.8 %all-to-all-start.2 = ((bf16[8,64,512]{2,1,0:T(8,128)(2,1)}), bf16[8,64,512]{2,1,0:T(8,128)(2,1)S(1)}, u32[]{:S(2)}, u32[]{:S(2)}) async-start(bf16[8,64,512]{2,1,0:T(8,128)(2,1)} %bitcast.95), calls=%async_computation.2 | async-start | bytes 1048576 | tf_op jit(solution)/shard_map/all_to_all | solution.py:54
  327.0 10.2 %copy-start.8 = (f32[8,128]{1,0:T(8,128)S(1)}, f32[8,128]{1,0:T(8,128)}, u32[]{:S(2)}) copy-start(f32[8,128]{1,0:T(8,128)} %param.20) | copy-start | bytes 12292
  331.7 20.9 %copy-start.10 = (s32[8,128]{1,0:T(8,128)S(1)}, s32[8,128]{1,0:T(8,128)}, u32[]{:S(2)}) copy-start(s32[8,128]{1,0:T(8,128)} %param.19) | copy-start | bytes 12292
  333.5 18.1 %all-to-all-start.3 = ((bf16[8,8,4096]{2,1,0:T(8,128)(2,1)}), bf16[8,8,4096]{2,1,0:T(8,128)(2,1)S(1)}, u32[]{:S(2)}, u32[]{:S(2)}) async-start(bf16[8,8,4096]{2,1,0:T(8,128)(2,1)} %bitcast_select_fusion), calls=%async_computation.3 | async-start | bytes 1048576 | tf_op jit(solution)/shard_map/all_to_all | solution.py:67
  337.1 48.4 %all-reduce.3.cloned.1.call-start = ((), (), s32[]{:S(2)}) async-start(), calls=%async_computation.8 | async-start | bytes 1048576 | tf_op jit(solution)/shard_map/psum | solution.py:22
  352.6 72.2 %collective-permute-start.2 = (bf16[64,4096]{1,0:T(8,128)(2,1)}, bf16[64,4096]{1,0:T(8,128)(2,1)}, u32[]{:S(2)}, u32[]{:S(2)}) collective-permute-start(bf16[64,4096]{1,0:T(8,128)(2,1)} %fusion.22), channel_id=1, source_target_pairs={{0,8},{8,16},{16,24},{1,9},{9,17},{17,25},{2,10},{10,18},{18,26},{... | collective-permute-start | bytes 1572872 | tf_op jit(solution)/shard_map/ppermute | solution.py:17
  386.7 39.0 %copy-start.2 = (bf16[64,4096]{1,0:T(8,128)(2,1)S(1)}, bf16[64,4096]{1,0:T(8,128)(2,1)}, u32[]{:S(2)}) copy-start(bf16[64,4096]{1,0:T(8,128)(2,1)} %all-reduce.3.cloned.1.call-done) | copy-start | bytes 1572868
  419.4 20.5 %all-to-all-start.4 = ((bf16[8,8,4096]{2,1,0:T(8,128)(2,1)}), bf16[8,8,4096]{2,1,0:T(8,128)(2,1)S(1)}, u32[]{:S(2)}, u32[]{:S(2)}) async-start(bf16[8,8,4096]{2,1,0:T(8,128)(2,1)} %bitcast.77), calls=%async_computation.4 | async-start | bytes 1048576 | tf_op jit(solution)/shard_map/all_to_all | solution.py:87
Sparse Core Ops, SparseCore 0:
  10.7 75.5 all-gather.3
  114.4 79.3 all-gather.5
  221.9 79.3 all-gather.7
  352.5 32.9 all-reduce.2
where the time goes:
time: 449 us
  waiting for transfers between devices  307 us (68%)
  blocking collectives  60.7 us (14%)
  matrix products  21.5 us (5%)
  starting transfers between devices  17.6 us (4%)
  other arithmetic  16.7 us (4%)
  between operations  16.2 us (4%)
  local copies, waits for them, and re-layouts  8.9 us (2%)
    all_gather x3, waiting for transfers between devices, on_device(): lax.all_gather(normed, 'dp', axis=0, tiled=True)  233 us
    all_to_all x2, blocking collectives, on_device(): lax.all_to_all(columns, 'dp', split_axis=0, concat_axis=1, tiled=True)  35 us
    psum x1, waiting for transfers between devices, from_root(): return lax.psum(kept, axis)  30.7 us
    psum x1, blocking collectives, on_device(): grad_whole = lax.psum(grad_terms, 'section').astype(jnp.bfloat16)  25.7 us
    dot_general x3, matrix products, on_device(): jnp.dot(lax.all_gather(normed, 'dp', axis=0, tiled=True), weight, preferr...  18.2 us
    all_to_all x1, waiting for transfers between devices, on_device(): lax.all_to_all(outbox, 'dp', split_axis=0, concat_axis=0, tiled=True)  14.3 us
    all_to_all x1, waiting for transfers between devices, on_device(): lax.all_to_all(grad_whole, 'dp', split_axis=0, concat_axis=0, tiled=True)  13.2 us
    all_to_all x1, waiting for transfers between devices, on_device(): lax.all_to_all(columns, 'dp', split_axis=0, concat_axis=1, tiled=True)  12.4 us
  transfers between devices with their start and end apart: 10, of which 9 were waited for; matrix products, arithmetic and copies ran while one was open for 3% of the time, Pallas kernels for 0%

commit v1 on v0

v1 whole, which is shorter than its diff:
```python
import jax
import jax.numpy as jnp
from jax import lax
from jax.sharding import PartitionSpec as P

SEQ = 128
TICKS = 3


epsilon = 1e-06
logit_scale = 20.0

AXES = ("section", "dp")


def on_device(
    fresh_batches,
    held_states,
    section_weight,
    section_gain,
    final_gain,
    cached_pool,
    route,
    queries,
    shortlist,
    teacher,
):
    section = lax.axis_index("section")
    sections = lax.axis_size("section")
    dp = lax.axis_index("dp")
    dps = lax.axis_size("dp")
    half = dps // 2
    side, place = dp % 2, dp // 2
    weight = section_weight[0]
    gain = section_gain[0]
    width, cols = weight.shape
    tok = held_states.shape[1]
    pair_rows = 2 * tok

    def send(x, hops):
        return lax.ppermute(
            x, AXES, [(a * dps + i, b * dps + (i ^ flip)) for a, b, flip in hops for i in range(dps)]
        )

    rows = cached_pool.shape[0]
    outbox = jnp.concatenate(
        [
            jnp.take(cached_pool, route[0], axis=0),
            jnp.broadcast_to(route[0].astype(jnp.bfloat16)[:, None], (rows, 128)),
        ],
        axis=1,
    )
    inbox = lax.all_to_all(outbox, "dp", split_axis=0, concat_axis=0, tiled=True)
    owner_queries = lax.all_gather(queries, "section", axis=0, tiled=True)

    gained = (weight.astype(jnp.float32) * gain[:, None]).astype(jnp.bfloat16)
    by_side = gained.reshape(half, 2, cols, cols)
    flips = jnp.where(section == 0, 0, place)
    mine_plain = lax.dynamic_index_in_dim(by_side, side, 1, keepdims=False)
    theirs_plain = lax.dynamic_index_in_dim(by_side, 1 - side, 1, keepdims=False)
    last_full = sections - 1 - TICKS
    theirs_plain = send(theirs_plain, [(a, a, 1) for a in range(sections - 1)])
    order = jnp.arange(half) ^ flips
    inner = half * cols

    def ordered(w):
        return jnp.take(w, order, axis=0).reshape(inner, cols)

    mine_late, theirs_late = ordered(mine_plain), ordered(theirs_plain)
    if last_full == 0:
        mine_first, theirs_first = mine_late, theirs_late
    else:
        mine_first = mine_plain.reshape(inner, cols)
        theirs_first = theirs_plain.reshape(inner, cols)

    def layer(states, mine, theirs, own_at, hops):
        wide = states.astype(jnp.float32)
        square = jnp.sum(wide * wide, axis=-1)
        other_square = send(square, hops)
        other = send(
            jnp.dot(states, theirs, preferred_element_type=jnp.float32).astype(jnp.bfloat16), hops
        )
        own = jnp.dot(states, mine, preferred_element_type=jnp.float32)
        inv_rms = lax.rsqrt((square + other_square) / width + epsilon)
        projected = ((own + other.astype(jnp.float32)) * inv_rms[:, None]).astype(jnp.bfloat16)
        kept = lax.dynamic_slice_in_dim(states, own_at * cols, cols, axis=1).astype(jnp.float32)
        return (kept + jax.nn.silu(projected.astype(jnp.float32))).astype(jnp.bfloat16)

    def token_order(block):
        piled = block.reshape(half, pair_rows, cols)
        return jnp.take(piled, jnp.arange(half) ^ place, axis=0).reshape(block.shape)

    entry = held_states[0]
    for i in range(TICKS - 1):
        entry = jnp.where(section == sections - TICKS + 1 + i, fresh_batches[i], entry)
    used = list(range(last_full + 1)) + list(range(sections - TICKS + 1, sections))
    entry = entry.reshape(tok, half, 2, cols)
    stay = lax.dynamic_index_in_dim(entry, side, 2, keepdims=False).reshape(tok, inner)
    leave = lax.dynamic_index_in_dim(entry, 1 - side, 2, keepdims=False).reshape(tok, inner)
    came = send(leave, [(a, a, 1) for a in used])
    pair = jnp.where(
        side == 0,
        jnp.concatenate([stay, came], axis=0),
        jnp.concatenate([came, stay], axis=0),
    )
    piles = [pair] + [send(pair, [(a, a, 2 * k) for a in used]) for k in range(1, half)]
    states = jnp.concatenate(piles, axis=0)
    fresh_states = [
        send(states, [(sections - TICKS + 1 + i, 0, 0)]) for i in range(TICKS - 1)
    ]
    block = layer(
        states, mine_first, theirs_first, place, [(a, a, 1) for a in range(last_full + 1)]
    )
    block = token_order(block)
    for tick in range(1, TICKS):
        top = last_full + tick
        piles = [send(block, [(a - 1, a, 2 * k) for a in range(1, top + 1)]) for k in range(half)]
        states = jnp.where(section == 0, fresh_states[tick - 1], jnp.concatenate(piles, axis=1))
        block = layer(
            states, mine_late, theirs_late, place - flips, [(a, a, 1) for a in range(top + 1)]
        )
        block = jnp.where(section == 0, token_order(block), block)
    tokens = lax.all_to_all(block, "dp", split_axis=0, concat_axis=1, tiled=True)
    shifted = send(tokens, [(a, a + 1, 0) for a in range(sections - 1)])
    held_out = jnp.where(section == 0, fresh_batches[TICKS - 1], shifted)

    def spread(x):
        return lax.all_to_all(
            jnp.broadcast_to(x[None], (dps, *x.shape)), "dp", split_axis=0, concat_axis=0
        )

    every = SEQ // tok
    ends = spread(held_states[0, tok - 1 :])[every - 1 :: every, 0]
    exits = []
    for tick in range(TICKS):
        wide = ends.astype(jnp.float32)
        inv_rms = lax.rsqrt(jnp.mean(wide * wide, axis=-1, keepdims=True) + epsilon)
        normed = (wide * inv_rms * gain).astype(jnp.bfloat16)
        projected = jnp.dot(normed, weight, preferred_element_type=jnp.float32).astype(jnp.bfloat16)
        kept = lax.dynamic_slice_in_dim(wide, dp * cols, cols, axis=1)
        piece = (kept + jax.nn.silu(projected.astype(jnp.float32))).astype(jnp.bfloat16)
        exits.append(piece)
        if tick < TICKS - 1:
            piece = send(piece, [(a, a + 1, 0) for a in range(sections - 1)])
            ends = jnp.concatenate(list(spread(piece)), axis=1)
    passages = ends.shape[0]
    exit_pieces = lax.all_gather(jnp.concatenate(exits, axis=0), "section", axis=0)[sections - 1]
    exit_rows = jnp.concatenate(list(spread(exit_pieces)), axis=1)
    scaled = exit_rows.astype(jnp.float32) * final_gain
    embedded = (
        scaled * lax.rsqrt(jnp.sum(scaled * scaled, axis=-1, keepdims=True) + epsilon)
    ).astype(jnp.bfloat16)

    per_peer = rows // dps
    source = jnp.arange(rows) // per_peer
    passage = source // every
    is_end = source % every == every - 1
    slot = inbox[:, width].astype(jnp.int32)
    replaced = is_end & (slot < TICKS)
    pick = jnp.where(replaced, slot * passages + passage, -1)
    chosen = (pick[:, None] == jnp.arange(TICKS * passages)).astype(jnp.bfloat16)
    received = jnp.where(
        replaced[:, None],
        jnp.dot(chosen, embedded, preferred_element_type=jnp.float32).astype(jnp.bfloat16),
        inbox[:, :width],
    )
    all_scores = lax.dot_general(
        queries, received, (((1,), (1,)), ((), ())), preferred_element_type=jnp.float32
    )
    listed = shortlist[..., None] == jnp.arange(rows, dtype=jnp.int32)
    student = jnp.sum(jnp.where(listed, all_scores[:, None, :], 0.0), axis=-1) * logit_scale
    student_log = jax.nn.log_softmax(student, axis=-1)
    teacher_log = jax.nn.log_softmax(teacher, axis=-1)
    teacher_prob = jnp.exp(teacher_log)
    losses = jnp.sum(teacher_prob * (teacher_log - student_log), axis=-1)
    logit_grad = logit_scale * (jnp.exp(student_log) - teacher_prob)
    row_grad = jnp.sum(jnp.where(listed, logit_grad[..., None], 0.0), axis=1)
    received_wide = received.astype(jnp.float32)
    owner_grads = lax.all_gather(row_grad, "section", axis=0, tiled=True)
    received_grad = jnp.dot(
        owner_grads.T, owner_queries.astype(jnp.float32), precision=lax.Precision.HIGHEST
    ).astype(jnp.bfloat16)
    query_grad = jnp.dot(row_grad, received_wide, precision=lax.Precision.HIGHEST)
    returned = lax.all_to_all(received_grad, "dp", split_axis=0, concat_axis=0, tiled=True)
    pool_grad = jnp.zeros(returned.shape, jnp.bfloat16).at[route[0]].set(returned)
    return (held_out[None], losses, query_grad, pool_grad)


def solution(mesh):
    return jax.shard_map(
        on_device,
        mesh=mesh,
        in_specs=(
            P(None, "dp", None),
            P("section", "dp", None),
            P("section", None, "dp"),
            P("section", None),
            P(),
            P("dp", None),
            P("dp", None),
            P(("section", "dp"), None),
            P(("section", "dp"), None),
            P(("section", "dp"), None),
        ),
        out_specs=(
            P("section", "dp", None),
            P(("section", "dp")),
            P(("section", "dp"), None),
            P("dp", None),
        ),
        check_vma=False,
    )
```

time: 449 us -> 324 us (0.72)
  waiting for transfers between devices: 307 us -> 90.5 us
  starting transfers between devices: 17.6 us -> 130 us
  blocking collectives: 60.7 us -> 16.2 us
  local copies, waits for them, and re-layouts: 8.9 us -> 29.6 us
  between operations: 16.2 us -> 1.59 us
  other arithmetic: 16.7 us -> 26.2 us
  matrix products: 21.5 us -> 28.3 us
    all_gather x3 -> x0, waiting for transfers between devices: 233 us -> none  [on_device(): lax.all_gather(normed, 'dp', axis=0, tiled=True)]
    ppermute x3 -> x24, starting transfers between devices: 4.76 us -> 64.7 us  [send(): lax.ppermute(x, AXES, [(a * dps + i, b * dps + (i ^ flip)) for a, b, flip...]
    all_to_all x2 -> x6, starting transfers between devices: 9.06 us -> 55 us  [the longest x1 27.3 us: on_device(): lax.all_to_all(block, 'dp', split_axis=0, concat_axis=1, tiled=True)]
    ppermute x3 -> x24, waiting for transfers between devices: 2.96 us -> 48.6 us  [send(): lax.ppermute(x, AXES, [(a * dps + i, b * dps + (i ^ flip)) for a, b, flip...]
    all_to_all x2 -> x0, blocking collectives: 35 us -> none  [on_device(): lax.all_to_all(columns, 'dp', split_axis=0, concat_axis=1, tiled=True)]
    psum x1 -> x0, waiting for transfers between devices: 30.7 us -> none  [from_root(): return lax.psum(kept, axis)]
    psum x1 -> x0, blocking collectives: 25.7 us -> none  [on_device(): grad_whole = lax.psum(grad_terms, 'section').astype(jnp.bfloat16)]
    all_to_all x2 -> x6, waiting for transfers between devices: 25.6 us -> 41.9 us  [the longest x4 23.5 us: spread(): lax.all_to_all(jnp.broadcast_to(x[None], (dps, *x.shape)), 'dp', split_ax...]
  transfers between devices with their start and end apart: 10 -> 31, of which waited for: 9 -> 15; matrix products, arithmetic and copies ran while one was open for 3% -> 23% of each run, Pallas kernels for 0% -> 0%
where the time goes in v1:
time: 324 us; the launch traced here: 322 us
  starting transfers between devices  130 us (40%)
  waiting for transfers between devices  90.5 us (28%)
  local copies, waits for them, and re-layouts  29.6 us (9%)
  matrix products  28.3 us (9%)
  other arithmetic  26.2 us (8%)
  blocking collectives  16.2 us (5%)
    ppermute x24, starting transfers between devices, send(): lax.ppermute(x, AXES, [(a * dps + i, b * dps + (i ^ flip)) for a, b, flip...  64.7 us
    ppermute x24, waiting for transfers between devices, send(): lax.ppermute(x, AXES, [(a * dps + i, b * dps + (i ^ flip)) for a, b, flip...  48.6 us
    all_to_all x1, starting transfers between devices, on_device(): lax.all_to_all(block, 'dp', split_axis=0, concat_axis=1, tiled=True)  27.3 us
    all_to_all x4, starting transfers between devices, spread(): lax.all_to_all(jnp.broadcast_to(x[None], (dps, *x.shape)), 'dp', split_ax...  24.1 us
    all_to_all x4, waiting for transfers between devices, spread(): lax.all_to_all(jnp.broadcast_to(x[None], (dps, *x.shape)), 'dp', split_ax...  23.5 us
    all_to_all x1, waiting for transfers between devices, on_device(): lax.all_to_all(received_grad, 'dp', split_axis=0, concat_axis=0, tiled=True)  12 us
    all_to_all x1, starting transfers between devices, on_device(): lax.all_to_all(outbox, 'dp', split_axis=0, concat_axis=0, tiled=True)  10.5 us
    dot_general x3, matrix products, layer(): own = jnp.dot(states, mine, preferred_element_type=jnp.float32)  8.69 us
  transfers between devices with their start and end apart: 31, of which 15 were waited for; matrix products, arithmetic and copies ran while one was open for 23% of the time, Pallas kernels for 0%

profile of v1, /device:TPU:0, one launch (start us, length us, event | category | flops | bytes accessed | tf_op | source)
XLA Modules:
  0.0 322.5 jit_solution(15851997710125030554)
XLA Ops:
  3.9 7.3 %all-to-all-start.2 = ((bf16[8,2,2048]{2,1,0:T(2,128)(2,1)}), bf16[8,2,2048]{2,1,0:T(2,128)(2,1)S(1)}, u32[]{:S(2)}, u32[]{:S(2)}) async-start(bf16[8,2,2048]{2,1,0:T(2,128)(2,1)} %reshape.406), calls=%async_computation.2 | async-start | bytes 131072 | tf_op jit(solution)/shard_map/all_to_all | solution.py:128
  17.5 3.9 %collective-permute-start.6 = (bf16[4,512,512]{2,1,0:T(8,128)(2,1)}, bf16[4,512,512]{2,1,0:T(8,128)(2,1)}, u32[]{:S(2)}, u32[]{:S(2)}) collective-permute-start(bf16[4,512,512]{2,1,0:T(8,128)(2,1)} %get-tuple-element.18), channel_id=1, source_target_pairs={{0,1},{1,0},{2,3},{3,2},{4,5},{5,4},{6,7},{7,6},{8,9},{9,8},{10,11... | collective-permute-start | bytes 6291464 | tf_op jit(solution)/shard_map/ppermute | solution.py:41
  41.3 6.0 %all-to-all-start.3 = ((bf16[8,4,512]{2,1,0:T(4,128)(2,1)}), bf16[8,4,512]{2,1,0:T(4,128)(2,1)S(1)}, u32[]{:S(2)}, u32[]{:S(2)}) async-start(bf16[8,4,512]{2,1,0:T(4,128)(2,1)} %broadcast_in_dim.126), calls=%async_computation.3 | async-start | bytes 65536 | tf_op jit(solution)/shard_map/all_to_all | solution.py:128
  47.3 22.6 %all-to-all-done.3 = bf16[8,4,512]{2,1,0:T(4,128)(2,1)S(1)} async-done(((bf16[8,4,512]{2,1,0:T(4,128)(2,1)}), bf16[8,4,512]{2,1,0:T(4,128)(2,1)S(1)}, u32[]{:S(2)}, u32[]{:S(2)}) %all-to-all-start.3) | async-done | bytes 32800 | tf_op jit(solution)/shard_map/all_to_all | solution.py:128
  77.7 5.7 %all-to-all-start.4 = ((bf16[8,4,512]{2,1,0:T(4,128)(2,1)}), bf16[8,4,512]{2,1,0:T(4,128)(2,1)S(1)}, u32[]{:S(2)}, u32[]{:S(2)}) async-start(bf16[8,4,512]{2,1,0:T(4,128)(2,1)} %broadcast_in_dim.127), calls=%async_computation.4 | async-start | bytes 65536 | tf_op jit(solution)/shard_map/all_to_all | solution.py:128
  83.4 5.8 %all_gather.15 = bf16[32,4096]{1,0:T(8,128)(2,1)S(1)} all-gather(bf16[8,4096]{1,0:T(8,128)(2,1)S(1)} %copy-done.10), channel_id=1, replica_groups=mesh['section'=4,'dp'=8] {'section'}, dimensions={0}, use_global_device_ids=true | all-gather | bytes 327680 | tf_op jit(solution)/shard_map/all_gather | solution.py:54
  94.6 4.3 %collective-permute-start.2 = (bf16[128,2048]{1,0:T(8,128)(2,1)S(1)}, bf16[128,2048]{1,0:T(8,128)(2,1)S(1)}, u32[]{:S(2)}, u32[]{:S(2)}) collective-permute-start(bf16[128,2048]{1,0:T(8,128)(2,1)S(1)} %maximum_select_fusion.2), channel_id=1, source_target_pairs={{0,4},{1,5},{2,6},{3,7},{4,0},{5,1},{6,2},{7,3},{16,20},{17,21},{1... | collective-permute-start | bytes 1572872 | tf_op jit(solution)/shard_map/ppermute | solution.py:41
  104.6 5.2 %all-gather.1 = bf16[4,12,512]{2,1,0:T(8,128)(2,1)S(1)} all-gather(bf16[1,12,512]{2,1,0:T(8,128)(2,1)S(1)} %maximum_bitcast_fusion), channel_id=2, replica_groups=mesh['section'=4,'dp'=8] {'section'}, dimensions={0}, use_global_device_ids=true | all-gather | bytes 61440 | tf_op jit(solution)/shard_map/all_gather | solution.py:147
  110.5 5.1 %all-to-all-start.5 = ((bf16[8,12,512]{2,1,0:T(8,128)(2,1)}), bf16[8,12,512]{2,1,0:T(8,128)(2,1)S(1)}, u32[]{:S(2)}, u32[]{:S(2)}) async-start(bf16[8,12,512]{2,1,0:T(8,128)(2,1)} %broadcast_in_dim.129), calls=%async_computation.5 | async-start | bytes 262144 | tf_op jit(solution)/shard_map/all_to_all | solution.py:128
  128.0 4.5 %convolution_convert_fusion.4 = bf16[512,512]{1,0:T(8,128)(2,1)} fusion(bf16[512,2048]{1,0:T(8,128)(2,1)} %get-tuple-element.16, bf16[2048,512]{1,0:T(8,128)(2,1)S(1)} %bitcast.209), kind=kOutput, calls=%fused_computation.46 | convolution fusion | flops 1074003968 | bytes 4718592 | tf_op jit(solution)/shard_map/dot_general | solution.py:81
  135.8 10.5 %all-to-all-start.1 = ((bf16[8,8,4224]{2,1,0:T(8,128)(2,1)}), bf16[8,8,4224]{2,1,0:T(8,128)(2,1)}, u32[]{:S(2)}, u32[]{:S(2)}) async-start(bf16[8,8,4224]{2,1,0:T(8,128)(2,1)} %pad_maximum_fusion.1), calls=%async_computation.1 | async-start | bytes 1081344 | tf_op jit(solution)/shard_map/all_to_all | solution.py:53
  165.3 5.0 %collective-permute-done.11 = bf16[512,512]{1,0:T(8,128)(2,1)S(1)} collective-permute-done((bf16[512,512]{1,0:T(8,128)(2,1)S(1)}, bf16[512,512]{1,0:T(8,128)(2,1)S(1)}, u32[]{:S(2)}, u32[]{:S(2)}) %collective-permute-start.11) | collective-permute-done | bytes 524320 | tf_op jit(solution)/shard_map/ppermute | solution.py:41
  170.3 5.6 %collective-permute-done.12 = bf16[512,512]{1,0:T(8,128)(2,1)S(1)} collective-permute-done((bf16[512,512]{1,0:T(8,128)(2,1)S(1)}, bf16[512,512]{1,0:T(8,128)(2,1)S(1)}, u32[]{:S(2)}, u32[]{:S(2)}) %collective-permute-start.12) | collective-permute-done | bytes 524320 | tf_op jit(solution)/shard_map/ppermute | solution.py:41
  179.5 3.9 %collective-permute-start.13 = (bf16[512,512]{1,0:T(8,128)(2,1)S(1)}, bf16[512,512]{1,0:T(8,128)(2,1)S(1)}, u32[]{:S(2)}, u32[]{:S(2)}) collective-permute-start(bf16[512,512]{1,0:T(8,128)(2,1)S(1)} %convolution_convert_fusion.3), channel_id=1, source_target_pairs={{0,1},{1,0},{2,3},{3,2},{4,5},{5,4},{6,7},{7,6},{8,9},{9,8},{10,11... | collective-permute-start | bytes 1572872 | tf_op jit(solution)/shard_map/ppermute | solution.py:41
  186.6 7.2 %collective-permute-done.14 = f32[512]{0:T(512)S(1)} collective-permute-done((f32[512]{0:T(512)S(1)}, f32[512]{0:T(512)S(1)}, u32[]{:S(2)}, u32[]{:S(2)}) %collective-permute-start.14) | collective-permute-done | bytes 2080 | tf_op jit(solution)/shard_map/ppermute | solution.py:41
  197.9 4.5 %collective-permute-start.15 = (bf16[512,512]{1,0:T(8,128)(2,1)S(1)}, bf16[512,512]{1,0:T(8,128)(2,1)S(1)}, u32[]{:S(2)}, u32[]{:S(2)}) collective-permute-start(bf16[512,512]{1,0:T(8,128)(2,1)S(1)} %bitcast_select_fusion.2), channel_id=1, source_target_pairs={{0,8},{1,9},{2,10},{3,11},{4,12},{5,13},{6,14},{7,15},{8,16},{9,17... | collective-permute-start | bytes 1572872 | tf_op jit(solution)/shard_map/ppermute | solution.py:41
  202.5 10.1 %collective-permute-start.16 = (bf16[512,512]{1,0:T(8,128)(2,1)S(1)}, bf16[512,512]{1,0:T(8,128)(2,1)S(1)}, u32[]{:S(2)}, u32[]{:S(2)}) collective-permute-start(bf16[512,512]{1,0:T(8,128)(2,1)S(1)} %bitcast_select_fusion.2), channel_id=1, source_target_pairs={{0,10},{1,11},{2,8},{3,9},{4,14},{5,15},{6,12},{7,13},{8,18},{9,19... | collective-permute-start | bytes 1572872 | tf_op jit(solution)/shard_map/ppermute | solution.py:41
  215.5 9.4 %collective-permute-done.16 = bf16[512,512]{1,0:T(8,128)(2,1)S(1)} collective-permute-done((bf16[512,512]{1,0:T(8,128)(2,1)S(1)}, bf16[512,512]{1,0:T(8,128)(2,1)S(1)}, u32[]{:S(2)}, u32[]{:S(2)}) %collective-permute-start.16) | collective-permute-done | bytes 524320 | tf_op jit(solution)/shard_map/ppermute | solution.py:41
  224.9 8.7 %collective-permute-done.17 = bf16[512,512]{1,0:T(8,128)(2,1)S(1)} collective-permute-done((bf16[512,512]{1,0:T(8,128)(2,1)S(1)}, bf16[512,512]{1,0:T(8,128)(2,1)S(1)}, u32[]{:S(2)}, u32[]{:S(2)}) %collective-permute-start.17) | collective-permute-done | bytes 524320 | tf_op jit(solution)/shard_map/ppermute | solution.py:41
  233.6 5.6 %collective-permute-done.18 = bf16[512,512]{1,0:T(8,128)(2,1)S(1)} collective-permute-done((bf16[512,512]{1,0:T(8,128)(2,1)S(1)}, bf16[512,512]{1,0:T(8,128)(2,1)S(1)}, u32[]{:S(2)}, u32[]{:S(2)}) %collective-permute-start.18) | collective-permute-done | bytes 524320 | tf_op jit(solution)/shard_map/ppermute | solution.py:41
  258.2 27.3 %all-to-all-start = ((bf16[8,64,512]{2,1,0:T(8,128)(2,1)}), bf16[8,64,512]{2,1,0:T(8,128)(2,1)S(1)}, u32[]{:S(2)}, u32[]{:S(2)}) async-start(bf16[8,64,512]{2,1,0:T(8,128)(2,1)} %bitcast.12), calls=%async_computation | async-start | bytes 1048576 | tf_op jit(solution)/shard_map/all_to_all | solution.py:123
  287.0 5.2 %all_gather.14 = f32[32,64]{1,0:T(8,128)S(1)} all-gather(f32[8,64]{1,0:T(8,128)S(1)} %select_reduce_fusion), channel_id=1, replica_groups=mesh['section'=4,'dp'=8] {'section'}, dimensions={0}, use_global_device_ids=true | all-gather | bytes 10240 | tf_op jit(solution)/shard_map/all_gather | solution.py:179
  293.6 6.4 %all-to-all-done = bf16[8,64,512]{2,1,0:T(8,128)(2,1)S(1)} async-done(((bf16[8,64,512]{2,1,0:T(8,128)(2,1)}), bf16[8,64,512]{2,1,0:T(8,128)(2,1)S(1)}, u32[]{:S(2)}, u32[]{:S(2)}) %all-to-all-start) | async-done | bytes 524320 | tf_op jit(solution)/shard_map/all_to_all | solution.py:123
  306.4 12.0 %all-to-all-done.6 = bf16[8,8,4096]{2,1,0:T(8,128)(2,1)S(1)} async-done(((bf16[8,8,4096]{2,1,0:T(8,128)(2,1)}), bf16[8,8,4096]{2,1,0:T(8,128)(2,1)S(1)}, u32[]{:S(2)}, u32[]{:S(2)}) %all-to-all-start.6) | async-done | bytes 524320 | tf_op jit(solution)/shard_map/all_to_all | solution.py:184
  (210 shorter events, 129.2 us)
Async XLA Ops:
  3.9 31.4 %all-to-all-start.2 = ((bf16[8,2,2048]{2,1,0:T(2,128)(2,1)}), bf16[8,2,2048]{2,1,0:T(2,128)(2,1)S(1)}, u32[]{:S(2)}, u32[]{:S(2)}) async-start(bf16[8,2,2048]{2,1,0:T(2,128)(2,1)} %reshape.406), calls=%async_computation.2 | async-start | bytes 131072 | tf_op jit(solution)/shard_map/all_to_all | solution.py:128
  17.5 103.5 %collective-permute-start.6 = (bf16[4,512,512]{2,1,0:T(8,128)(2,1)}, bf16[4,512,512]{2,1,0:T(8,128)(2,1)}, u32[]{:S(2)}, u32[]{:S(2)}) collective-permute-start(bf16[4,512,512]{2,1,0:T(8,128)(2,1)} %get-tuple-element.18), channel_id=1, source_target_pairs={{0,1},{1,0},{2,3},{3,2},{4,5},{5,4},{6,7},{7,6},{8,9},{9,8},{10,11... | collective-permute-start | bytes 6291464 | tf_op jit(solution)/shard_map/ppermute | solution.py:41
  29.0 61.4 %collective-permute-start = (bf16[64,2048]{1,0:T(8,128)(2,1)}, bf16[64,2048]{1,0:T(8,128)(2,1)}, u32[]{:S(2)}, u32[]{:S(2)}) collective-permute-start(bf16[64,2048]{1,0:T(8,128)(2,1)} %bitcast.57), channel_id=1, source_target_pairs={{0,1},{1,0},{2,3},{3,2},{4,5},{5,4},{6,7},{7,6},{16,17},{17,16},{1... | collective-permute-start | bytes 786440 | tf_op jit(solution)/shard_map/ppermute | solution.py:41
  41.3 28.6 %all-to-all-start.3 = ((bf16[8,4,512]{2,1,0:T(4,128)(2,1)}), bf16[8,4,512]{2,1,0:T(4,128)(2,1)S(1)}, u32[]{:S(2)}, u32[]{:S(2)}) async-start(bf16[8,4,512]{2,1,0:T(4,128)(2,1)} %broadcast_in_dim.126), calls=%async_computation.3 | async-start | bytes 65536 | tf_op jit(solution)/shard_map/all_to_all | solution.py:128
  77.7 12.4 %all-to-all-start.4 = ((bf16[8,4,512]{2,1,0:T(4,128)(2,1)}), bf16[8,4,512]{2,1,0:T(4,128)(2,1)S(1)}, u32[]{:S(2)}, u32[]{:S(2)}) async-start(bf16[8,4,512]{2,1,0:T(4,128)(2,1)} %broadcast_in_dim.127), calls=%async_computation.4 | async-start | bytes 65536 | tf_op jit(solution)/shard_map/all_to_all | solution.py:128
  91.5 24.1 %collective-permute-start.1 = (bf16[128,2048]{1,0:T(8,128)(2,1)S(1)}, bf16[128,2048]{1,0:T(8,128)(2,1)S(1)}, u32[]{:S(2)}, u32[]{:S(2)}) collective-permute-start(bf16[128,2048]{1,0:T(8,128)(2,1)S(1)} %maximum_select_fusion.2), channel_id=1, source_target_pairs={{0,2},{1,3},{2,0},{3,1},{4,6},{5,7},{6,4},{7,5},{16,18},{17,19},{1... | collective-permute-start | bytes 1572872 | tf_op jit(solution)/shard_map/ppermute | solution.py:41
  94.6 23.3 %collective-permute-start.2 = (bf16[128,2048]{1,0:T(8,128)(2,1)S(1)}, bf16[128,2048]{1,0:T(8,128)(2,1)S(1)}, u32[]{:S(2)}, u32[]{:S(2)}) collective-permute-start(bf16[128,2048]{1,0:T(8,128)(2,1)S(1)} %maximum_select_fusion.2), channel_id=1, source_target_pairs={{0,4},{1,5},{2,6},{3,7},{4,0},{5,1},{6,2},{7,3},{16,20},{17,21},{1... | collective-permute-start | bytes 1572872 | tf_op jit(solution)/shard_map/ppermute | solution.py:41
  98.8 19.0 %collective-permute-start.3 = (bf16[128,2048]{1,0:T(8,128)(2,1)S(1)}, bf16[128,2048]{1,0:T(8,128)(2,1)S(1)}, u32[]{:S(2)}, u32[]{:S(2)}) collective-permute-start(bf16[128,2048]{1,0:T(8,128)(2,1)S(1)} %maximum_select_fusion.2), channel_id=1, source_target_pairs={{0,6},{1,7},{2,4},{3,5},{4,2},{5,3},{6,0},{7,1},{16,22},{17,23},{1... | collective-permute-start | bytes 1572872 | tf_op jit(solution)/shard_map/ppermute | solution.py:41
  110.5 25.3 %all-to-all-start.5 = ((bf16[8,12,512]{2,1,0:T(8,128)(2,1)}), bf16[8,12,512]{2,1,0:T(8,128)(2,1)S(1)}, u32[]{:S(2)}, u32[]{:S(2)}) async-start(bf16[8,12,512]{2,1,0:T(8,128)(2,1)} %broadcast_in_dim.129), calls=%async_computation.5 | async-start | bytes 262144 | tf_op jit(solution)/shard_map/all_to_all | solution.py:128
  119.4 44.5 %collective-permute-start.5 = (bf16[512,2048]{1,0:T(8,128)(2,1)}, bf16[512,2048]{1,0:T(8,128)(2,1)}, u32[]{:S(2)}, u32[]{:S(2)}) collective-permute-start(bf16[512,2048]{1,0:T(8,128)(2,1)} %get-tuple-element.16), channel_id=1, source_target_pairs={{16,0},{17,1},{18,2},{19,3},{20,4},{21,5},{22,6},{23,7}} | collective-permute-start | bytes 6291464 | tf_op jit(solution)/shard_map/ppermute | solution.py:41
  132.4 20.1 %collective-permute-start.7 = (bf16[512,512]{1,0:T(8,128)(2,1)}, bf16[512,512]{1,0:T(8,128)(2,1)}, u32[]{:S(2)}, u32[]{:S(2)}) collective-permute-start(bf16[512,512]{1,0:T(8,128)(2,1)} %convolution_convert_fusion.4), channel_id=1, source_target_pairs={{0,1},{1,0},{2,3},{3,2},{4,5},{5,4},{6,7},{7,6}} | collective-permute-start | bytes 1572872 | tf_op jit(solution)/shard_map/ppermute | solution.py:41
  135.8 109.3 %all-to-all-start.1 = ((bf16[8,8,4224]{2,1,0:T(8,128)(2,1)}), bf16[8,8,4224]{2,1,0:T(8,128)(2,1)}, u32[]{:S(2)}, u32[]{:S(2)}) async-start(bf16[8,8,4224]{2,1,0:T(8,128)(2,1)} %pad_maximum_fusion.1), calls=%async_computation.1 | async-start | bytes 1081344 | tf_op jit(solution)/shard_map/all_to_all | solution.py:53
  158.0 12.3 %collective-permute-start.11 = (bf16[512,512]{1,0:T(8,128)(2,1)S(1)}, bf16[512,512]{1,0:T(8,128)(2,1)S(1)}, u32[]{:S(2)}, u32[]{:S(2)}) collective-permute-start(bf16[512,512]{1,0:T(8,128)(2,1)S(1)} %bitcast.217), channel_id=1, source_target_pairs={{0,12},{1,13},{2,14},{3,15},{4,8},{5,9},{6,10},{7,11}} | collective-permute-start | bytes 1572872 | tf_op jit(solution)/shard_map/ppermute | solution.py:41
  159.3 16.6 %collective-permute-start.12 = (bf16[512,512]{1,0:T(8,128)(2,1)S(1)}, bf16[512,512]{1,0:T(8,128)(2,1)S(1)}, u32[]{:S(2)}, u32[]{:S(2)}) collective-permute-start(bf16[512,512]{1,0:T(8,128)(2,1)S(1)} %bitcast.218), channel_id=1, source_target_pairs={{0,14},{1,15},{2,12},{3,13},{4,10},{5,11},{6,8},{7,9}} | collective-permute-start | bytes 1572872 | tf_op jit(solution)/shard_map/ppermute | solution.py:41
  160.6 15.3 %collective-permute-start.9 = (bf16[512,512]{1,0:T(8,128)(2,1)S(1)}, bf16[512,512]{1,0:T(8,128)(2,1)S(1)}, u32[]{:S(2)}, u32[]{:S(2)}) collective-permute-start(bf16[512,512]{1,0:T(8,128)(2,1)S(1)} %bitcast.219), channel_id=1, source_target_pairs={{0,8},{1,9},{2,10},{3,11},{4,12},{5,13},{6,14},{7,15}} | collective-permute-start | bytes 1572872 | tf_op jit(solution)/shard_map/ppermute | solution.py:41
  163.9 51.6 %collective-permute-start.4 = (bf16[512,2048]{1,0:T(8,128)(2,1)}, bf16[512,2048]{1,0:T(8,128)(2,1)S(1)}, u32[]{:S(2)}, u32[]{:S(2)}) collective-permute-start(bf16[512,2048]{1,0:T(8,128)(2,1)} %get-tuple-element.16), channel_id=1, source_target_pairs={{24,0},{25,1},{26,2},{27,3},{28,4},{29,5},{30,6},{31,7}} | collective-permute-start | bytes 6291464 | tf_op jit(solution)/shard_map/ppermute | solution.py:41
  179.5 14.3 %collective-permute-start.13 = (bf16[512,512]{1,0:T(8,128)(2,1)S(1)}, bf16[512,512]{1,0:T(8,128)(2,1)S(1)}, u32[]{:S(2)}, u32[]{:S(2)}) collective-permute-start(bf16[512,512]{1,0:T(8,128)(2,1)S(1)} %convolution_convert_fusion.3), channel_id=1, source_target_pairs={{0,1},{1,0},{2,3},{3,2},{4,5},{5,4},{6,7},{7,6},{8,9},{9,8},{10,11... | collective-permute-start | bytes 1572872 | tf_op jit(solution)/shard_map/ppermute | solution.py:41
  197.9 17.5 %collective-permute-start.15 = (bf16[512,512]{1,0:T(8,128)(2,1)S(1)}, bf16[512,512]{1,0:T(8,128)(2,1)S(1)}, u32[]{:S(2)}, u32[]{:S(2)}) collective-permute-start(bf16[512,512]{1,0:T(8,128)(2,1)S(1)} %bitcast_select_fusion.2), channel_id=1, source_target_pairs={{0,8},{1,9},{2,10},{3,11},{4,12},{5,13},{6,14},{7,15},{8,16},{9,17... | collective-permute-start | bytes 1572872 | tf_op jit(solution)/shard_map/ppermute | solution.py:41
  202.5 22.4 %collective-permute-start.16 = (bf16[512,512]{1,0:T(8,128)(2,1)S(1)}, bf16[512,512]{1,0:T(8,128)(2,1)S(1)}, u32[]{:S(2)}, u32[]{:S(2)}) collective-permute-start(bf16[512,512]{1,0:T(8,128)(2,1)S(1)} %bitcast_select_fusion.2), channel_id=1, source_target_pairs={{0,10},{1,11},{2,8},{3,9},{4,14},{5,15},{6,12},{7,13},{8,18},{9,19... | collective-permute-start | bytes 1572872 | tf_op jit(solution)/shard_map/ppermute | solution.py:41
  212.5 21.0 %collective-permute-start.17 = (bf16[512,512]{1,0:T(8,128)(2,1)S(1)}, bf16[512,512]{1,0:T(8,128)(2,1)S(1)}, u32[]{:S(2)}, u32[]{:S(2)}) collective-permute-start(bf16[512,512]{1,0:T(8,128)(2,1)S(1)} %bitcast_select_fusion.2), channel_id=1, source_target_pairs={{0,12},{1,13},{2,14},{3,15},{4,8},{5,9},{6,10},{7,11},{8,20},{9,21... | collective-permute-start | bytes 1572872 | tf_op jit(solution)/shard_map/ppermute | solution.py:41
  213.9 25.3 %collective-permute-start.18 = (bf16[512,512]{1,0:T(8,128)(2,1)S(1)}, bf16[512,512]{1,0:T(8,128)(2,1)S(1)}, u32[]{:S(2)}, u32[]{:S(2)}) collective-permute-start(bf16[512,512]{1,0:T(8,128)(2,1)S(1)} %bitcast_select_fusion.2), channel_id=1, source_target_pairs={{0,14},{1,15},{2,12},{3,13},{4,10},{5,11},{6,8},{7,9},{8,22},{9,23... | collective-permute-start | bytes 1572872 | tf_op jit(solution)/shard_map/ppermute | solution.py:41
  258.2 41.9 %all-to-all-start = ((bf16[8,64,512]{2,1,0:T(8,128)(2,1)}), bf16[8,64,512]{2,1,0:T(8,128)(2,1)S(1)}, u32[]{:S(2)}, u32[]{:S(2)}) async-start(bf16[8,64,512]{2,1,0:T(8,128)(2,1)} %bitcast.12), calls=%async_computation | async-start | bytes 1048576 | tf_op jit(solution)/shard_map/all_to_all | solution.py:123
  300.1 18.3 %all-to-all-start.6 = ((bf16[8,8,4096]{2,1,0:T(8,128)(2,1)}), bf16[8,8,4096]{2,1,0:T(8,128)(2,1)S(1)}, u32[]{:S(2)}, u32[]{:S(2)}) async-start(bf16[8,8,4096]{2,1,0:T(8,128)(2,1)} %fusion.2), calls=%async_computation.6 | async-start | bytes 1048576 | tf_op jit(solution)/shard_map/all_to_all | solution.py:184
  303.7 16.8 %collective-permute-start.21 = (bf16[64,4096]{1,0:T(8,128)(2,1)S(1)}, bf16[64,4096]{1,0:T(8,128)(2,1)S(1)}, u32[]{:S(2)}, u32[]{:S(2)}) collective-permute-start(bf16[64,4096]{1,0:T(8,128)(2,1)S(1)} %bitcast.215), channel_id=1, source_target_pairs={{0,8},{1,9},{2,10},{3,11},{4,12},{5,13},{6,14},{7,15},{8,16},{9,17... | collective-permute-start | bytes 1572872 | tf_op jit(solution)/shard_map/ppermute | solution.py:41
  (31 other events, 386.0 us)

commit v2 on v1

v2 whole, which is shorter than its diff:
```python
import jax
import jax.numpy as jnp
from jax import lax
from jax.sharding import PartitionSpec as P


SEQ = 128
TICKS = 3


epsilon = 1e-06
logit_scale = 20.0

AXES = ("section", "dp")


def on_device(
    fresh_batches,
    held_states,
    section_weight,
    section_gain,
    final_gain,
    cached_pool,
    route,
    queries,
    shortlist,
    teacher,
):
    section = lax.axis_index("section")
    sections = lax.axis_size("section")
    dp = lax.axis_index("dp")
    dps = lax.axis_size("dp")
    half = dps // 2
    side, place = dp % 2, dp // 2
    weight = section_weight[0]
    gain = section_gain[0]
    width, cols = weight.shape
    tok = held_states.shape[1]
    pair_rows = 2 * tok

    def send(x, hops):
        return lax.ppermute(
            x, AXES, [(a * dps + i, b * dps + (i ^ flip)) for a, b, flip in hops for i in range(dps)]
        )

    def rows_at(x, index):
        return x.at[index].get(mode="promise_in_bounds")

    by_block = weight.reshape(dps, cols, cols)
    gain_block = gain.reshape(dps, cols, 1)
    flips = jnp.where(section == 0, 0, place)
    inner = half * cols
    last_full = sections - 1 - TICKS

    def gained(order, at):
        index = 2 * order + at
        wide = rows_at(by_block, index).astype(jnp.float32) * rows_at(gain_block, index)
        return wide.astype(jnp.bfloat16).reshape(inner, cols)

    def split_weights(order, firsts):
        mine, theirs = gained(order, side), gained(order, 1 - side)
        rest = [a for a in range(sections - 1) if a not in firsts]
        came = send(theirs, [(a, a, 1) for a in firsts])
        if rest:
            later = send(theirs, [(a, a, 1) for a in rest])
        else:
            later = came
        return mine, came, jnp.where(section <= max(firsts), came, later)

    mine_late, theirs_first, theirs_late = split_weights(
        jnp.arange(half) ^ flips, list(range(last_full + 1))
    )
    mine_first = mine_late
    if last_full > 0:
        mine_first, _, theirs_first = split_weights(
            jnp.arange(half), list(range(last_full + 1))
        )

    entry = held_states[0]
    for i in range(TICKS - 1):
        entry = jnp.where(section == sections - TICKS + 1 + i, fresh_batches[i], entry)
    used = list(range(last_full + 1)) + list(range(sections - TICKS + 1, sections))
    pieces = [entry[:, k * cols : (k + 1) * cols] for k in range(dps)]
    even, odd = jnp.concatenate(pieces[0::2], axis=1), jnp.concatenate(pieces[1::2], axis=1)
    stay, leave = jnp.where(side == 0, even, odd), jnp.where(side == 0, odd, even)
    came = send(leave, [(a, a, 1) for a in used])
    pair = jnp.where(
        side == 0,
        jnp.concatenate([stay, came], axis=0),
        jnp.concatenate([came, stay], axis=0),
    )
    piles = [pair] + [send(pair, [(a, a, 2 * k) for a in used]) for k in range(1, half)]
    states = jnp.concatenate(piles, axis=0)

    rows = cached_pool.shape[0]
    per_peer = rows // dps
    last_token = held_states[0, tok - 1].reshape(1, per_peer, width // per_peer)
    outbox = jnp.concatenate(
        [
            rows_at(cached_pool, route[0]).reshape(dps, per_peer, width),
            jnp.broadcast_to(last_token, (dps, per_peer, width // per_peer)),
            jnp.broadcast_to(
                route[0].astype(jnp.bfloat16).reshape(dps, per_peer, 1), (dps, per_peer, 128)
            ),
        ],
        axis=2,
    )
    inbox = lax.all_to_all(outbox, "dp", split_axis=0, concat_axis=0)
    owner_queries = lax.all_gather(queries, "section", axis=0, tiled=True)

    def layer(states, mine, theirs, own_at, hops):
        wide = states.astype(jnp.float32)
        square = jnp.sum(wide * wide, axis=-1)
        other_square = send(square, hops)
        part = jnp.dot(states, theirs, preferred_element_type=jnp.float32).astype(jnp.bfloat16)
        other = send(part, hops)
        own = jnp.dot(states, mine, preferred_element_type=jnp.float32)
        inv_rms = lax.rsqrt((square + other_square) / width + epsilon)
        projected = ((own + other.astype(jnp.float32)) * inv_rms[:, None]).astype(jnp.bfloat16)
        kept = lax.dynamic_slice_in_dim(states, own_at * cols, cols, axis=1).astype(jnp.float32)
        return (kept + jax.nn.silu(projected.astype(jnp.float32))).astype(jnp.bfloat16)

    def reorder(block, flip):
        piled = block.reshape(half, pair_rows, cols)
        return rows_at(piled, jnp.arange(half) ^ flip).reshape(block.shape)

    fresh_states = []
    for i in range(TICKS - 1):
        fresh_states.append(send(states, [(sections - TICKS + 1 + i, 0, 0)]))
    block = layer(
        states, mine_first, theirs_first, place, [(a, a, 1) for a in range(last_full + 1)]
    )
    block = reorder(block, place)
    for tick in range(1, TICKS):
        top = last_full + tick
        if tick == 1:
            piles = [
                send(block, [(a - 1, a, 2 * k) for a in range(1, top + 1)])
                for k in range(half)
            ]
        else:
            block = send(block, [(a - 1, a, 0) for a in range(1, top + 1)])
            piles = [block] + [
                send(block, [(a, a, 2 * k) for a in range(1, top + 1)])
                for k in range(1, half)
            ]
        states = jnp.where(section == 0, fresh_states[tick - 1], jnp.concatenate(piles, axis=1))
        block = layer(
            states, mine_late, theirs_late, place - flips, [(a, a, 1) for a in range(top + 1)]
        )
        block = reorder(block, place - flips)
    tokens = lax.all_to_all(block, "dp", split_axis=0, concat_axis=1, tiled=True)
    shifted = send(tokens, [(a, a + 1, 0) for a in range(sections - 1)])
    held_out = jnp.where(section == 0, fresh_batches[TICKS - 1], shifted)

    def spread(x):
        pieces = lax.all_to_all(
            jnp.broadcast_to(x[None], (dps, *x.shape)), "dp", split_axis=0, concat_axis=0
        )
        return jnp.transpose(pieces, (1, 0, 2)).reshape(x.shape[0], width)

    every = SEQ // tok
    ends = inbox[every - 1 :: every, :, width : width + width // per_peer].reshape(-1, width)
    exits = []
    for tick in range(TICKS):
        wide = ends.astype(jnp.float32)
        inv_rms = lax.rsqrt(jnp.mean(wide * wide, axis=-1, keepdims=True) + epsilon)
        normed = (wide * inv_rms * gain).astype(jnp.bfloat16)
        projected = jnp.dot(normed, weight, preferred_element_type=jnp.float32)
        projected = projected.astype(jnp.bfloat16).astype(jnp.float32)
        kept = lax.dynamic_slice_in_dim(wide, dp * cols, cols, axis=1)
        piece = (kept + jax.nn.silu(projected)).astype(jnp.bfloat16)
        exits.append(piece)
        if tick < TICKS - 1:
            piece = send(piece, [(a, a + 1, 0) for a in range(sections - 1)])
            ends = spread(piece)
    passages = ends.shape[0]
    exit_pieces = lax.all_gather(jnp.concatenate(exits, axis=0), "section", axis=0)
    exit_rows = spread(exit_pieces[sections - 1])
    scaled = exit_rows.astype(jnp.float32) * final_gain
    embedded = (
        scaled * lax.rsqrt(jnp.sum(scaled * scaled, axis=-1, keepdims=True) + epsilon)
    ).astype(jnp.bfloat16)

    source = jnp.arange(rows) // per_peer
    passage = source // every
    is_end = source % every == every - 1
    slot = inbox[:, :, width + width // per_peer].reshape(rows).astype(jnp.int32)
    replaced = is_end & (slot < TICKS)
    pick = jnp.where(replaced, slot * passages + passage, -1)
    chosen = (pick[:, None] == jnp.arange(TICKS * passages)).astype(jnp.bfloat16)
    received = jnp.where(
        replaced[:, None],
        jnp.dot(chosen, embedded, preferred_element_type=jnp.float32).astype(jnp.bfloat16),
        inbox[:, :, :width].reshape(rows, width),
    )
    all_scores = lax.dot_general(
        queries, received, (((1,), (1,)), ((), ())), preferred_element_type=jnp.float32
    )
    listed = shortlist[..., None] == jnp.arange(rows, dtype=jnp.int32)
    student = jnp.sum(jnp.where(listed, all_scores[:, None, :], 0.0), axis=-1) * logit_scale
    student_log = jax.nn.log_softmax(student, axis=-1)
    teacher_log = jax.nn.log_softmax(teacher, axis=-1)
    teacher_prob = jnp.exp(teacher_log)
    losses = jnp.sum(teacher_prob * (teacher_log - student_log), axis=-1)
    logit_grad = logit_scale * (jnp.exp(student_log) - teacher_prob)
    row_grad = jnp.sum(jnp.where(listed, logit_grad[..., None], 0.0), axis=1)
    received_wide = received.astype(jnp.float32)
    owner_grads = lax.all_gather(row_grad, "section", axis=0, tiled=True)
    received_grad = jnp.dot(
        owner_grads.T, owner_queries.astype(jnp.float32), precision=lax.Precision.HIGHEST
    ).astype(jnp.bfloat16)
    query_grad = jnp.dot(row_grad, received_wide, precision=lax.Precision.HIGHEST)
    returned = lax.all_to_all(received_grad, "dp", split_axis=0, concat_axis=0, tiled=True)
    pool_grad = jnp.zeros(returned.shape, jnp.bfloat16).at[route[0]].set(returned)
    return (held_out[None], losses, query_grad, pool_grad)


def solution(mesh):
    return jax.shard_map(
        on_device,
        mesh=mesh,
        in_specs=(
            P(None, "dp", None),
            P("section", "dp", None),
            P("section", None, "dp"),
            P("section", None),
            P(),
            P("dp", None),
            P("dp", None),
            P(("section", "dp"), None),
            P(("section", "dp"), None),
            P(("section", "dp"), None),
        ),
        out_specs=(
            P("section", "dp", None),
            P(("section", "dp")),
            P(("section", "dp"), None),
            P("dp", None),
        ),
        check_vma=False,
    )
```

time: 324 us -> 302 us (0.932)
  starting transfers between devices: 130 us -> 83.1 us
  blocking collectives: 16.2 us -> 42.6 us
  waiting for transfers between devices: 90.5 us -> 100 us
  local copies, waits for them, and re-layouts: 29.6 us -> 22.9 us
    all_gather x1, blocking collectives: 5.21 us -> 31.2 us  [on_device(): owner_grads = lax.all_gather(row_grad, 'section', axis=0, tiled=True)]
    all_to_all x1, starting transfers between devices: 27.3 us -> 3.49 us  [on_device(): lax.all_to_all(block, 'dp', split_axis=0, concat_axis=1, tiled=True)]
    ppermute x24 -> x25, waiting for transfers between devices: 48.6 us -> 71.9 us  [send(): lax.ppermute(x, AXES, [(a * dps + i, b * dps + (i ^ flip)) for a, b, flip...]
    all_to_all x4 -> x3, starting transfers between devices: 24.1 us -> 10.5 us  [spread(): lax.all_to_all(jnp.broadcast_to(x[None], (dps, *x.shape)), 'dp', split_ax...]
    ppermute x24 -> x25, starting transfers between devices: 64.7 us -> 56.9 us  [send(): lax.ppermute(x, AXES, [(a * dps + i, b * dps + (i ^ flip)) for a, b, flip...]
    all_to_all x4 -> x3, waiting for transfers between devices: 23.5 us -> 16.4 us  [spread(): lax.all_to_all(jnp.broadcast_to(x[None], (dps, *x.shape)), 'dp', split_ax...]
    unnamed x75 -> x51, local copies, waits for them, and re-layouts: 7.59 us -> 0.88 us
    all_to_all x1, waiting for transfers between devices: 6.43 us -> 0.01 us  [on_device(): lax.all_to_all(block, 'dp', split_axis=0, concat_axis=1, tiled=True)]
  transfers between devices with their start and end apart: 31 -> 31, of which waited for: 15 -> 10; matrix products, arithmetic and copies ran while one was open for 23% -> 18% of each run, Pallas kernels for 0% -> 0%
where the time goes in v2:
time: 302 us; the launch traced here: 300 us
  waiting for transfers between devices  100 us (33%)
  starting transfers between devices  83.1 us (28%)
  blocking collectives  42.6 us (14%)
  matrix products  26.5 us (9%)
  other arithmetic  23.2 us (8%)
  local copies, waits for them, and re-layouts  22.9 us (8%)
    ppermute x25, waiting for transfers between devices, send(): lax.ppermute(x, AXES, [(a * dps + i, b * dps + (i ^ flip)) for a, b, flip...  71.9 us
    ppermute x25, starting transfers between devices, send(): lax.ppermute(x, AXES, [(a * dps + i, b * dps + (i ^ flip)) for a, b, flip...  56.9 us
    all_gather x1, blocking collectives, on_device(): owner_grads = lax.all_gather(row_grad, 'section', axis=0, tiled=True)  31.2 us
    all_to_all x3, waiting for transfers between devices, spread(): lax.all_to_all(jnp.broadcast_to(x[None], (dps, *x.shape)), 'dp', split_ax...  16.4 us
    gather x8, local copies, waits for them, and re-layouts, rows_at(): return x.at[index].get(mode='promise_in_bounds')  13.5 us
    all_to_all x1, waiting for transfers between devices, on_device(): lax.all_to_all(received_grad, 'dp', split_axis=0, concat_axis=0, tiled=True)  12 us
    all_to_all x3, starting transfers between devices, spread(): lax.all_to_all(jnp.broadcast_to(x[None], (dps, *x.shape)), 'dp', split_ax...  10.5 us
    dot_general x3, matrix products, layer(): jnp.dot(states, theirs, preferred_element_type=jnp.float32)  9.41 us
  transfers between devices with their start and end apart: 31, of which 10 were waited for; matrix products, arithmetic and copies ran while one was open for 18% of the time, Pallas kernels for 0%

profile of v2, /device:TPU:0, one launch (start us, length us, event | category | flops | bytes accessed | tf_op | source)
XLA Modules:
  0.0 300.2 jit_solution(13459054173710699628)
XLA Ops:
  7.9 4.9 %collective-permute-start.6 = (bf16[2048,512]{1,0:T(8,128)(2,1)}, bf16[2048,512]{1,0:T(8,128)(2,1)}, u32[]{:S(2)}, u32[]{:S(2)}) collective-permute-start(bf16[2048,512]{1,0:T(8,128)(2,1)} %fusion.2), channel_id=1, source_target_pairs={{0,1},{1,0},{2,3},{3,2},{4,5},{5,4},{6,7},{7,6}} | collective-permute-start | bytes 6291464 | tf_op jit(solution)/shard_map/ppermute | solution.py:42
  21.9 6.3 %all-to-all-start.1 = ((bf16[8,8,4736]{2,1,0:T(8,128)(2,1)}), bf16[8,8,4736]{2,1,0:T(8,128)(2,1)S(1)}, u32[]{:S(2)}, u32[]{:S(2)}) async-start(bf16[8,8,4736]{2,1,0:T(8,128)(2,1)} %pad_maximum_fusion.1), calls=%async_computation.1 | async-start | bytes 1212416 | tf_op jit(solution)/shard_map/all_to_all | solution.py:108
  32.1 36.0 %collective-permute-done = bf16[64,2048]{1,0:T(8,128)(2,1)} collective-permute-done((bf16[64,2048]{1,0:T(8,128)(2,1)}, bf16[64,2048]{1,0:T(8,128)(2,1)}, u32[]{:S(2)}, u32[]{:S(2)}) %collective-permute-start) | collective-permute-done | bytes 262176 | tf_op jit(solution)/shard_map/ppermute | solution.py:42
  69.2 6.0 %collective-permute-start.3 = (bf16[128,2048]{1,0:T(8,128)(2,1)S(1)}, bf16[128,2048]{1,0:T(8,128)(2,1)S(1)}, u32[]{:S(2)}, u32[]{:S(2)}) collective-permute-start(bf16[128,2048]{1,0:T(8,128)(2,1)S(1)} %maximum_select_fusion.2), channel_id=1, source_target_pairs={{0,6},{1,7},{2,4},{3,5},{4,2},{5,3},{6,0},{7,1},{16,22},{17,23},{1... | collective-permute-start | bytes 1572872 | tf_op jit(solution)/shard_map/ppermute | solution.py:42
  82.5 16.2 %collective-permute-done.2 = bf16[128,2048]{1,0:T(8,128)(2,1)S(1)} collective-permute-done((bf16[128,2048]{1,0:T(8,128)(2,1)S(1)}, bf16[128,2048]{1,0:T(8,128)(2,1)S(1)}, u32[]{:S(2)}, u32[]{:S(2)}) %collective-permute-start.2) | collective-permute-done | bytes 524320 | tf_op jit(solution)/shard_map/ppermute | solution.py:42
  101.6 3.4 %collective-permute-start.8 = (f32[512]{0:T(512)S(1)}, f32[512]{0:T(512)S(1)}, u32[]{:S(2)}, u32[]{:S(2)}) collective-permute-start(f32[512]{0:T(512)S(1)} %get-tuple-element.11), channel_id=1, source_target_pairs={{0,1},{1,0},{2,3},{3,2},{4,5},{5,4},{6,7},{7,6}} | collective-permute-start | bytes 6152 | tf_op jit(solution)/shard_map/ppermute | solution.py:42
  111.3 3.8 %all-to-all-start.2 = ((bf16[8,4,512]{2,1,0:T(4,128)(2,1)}), bf16[8,4,512]{2,1,0:T(4,128)(2,1)S(1)}, u32[]{:S(2)}, u32[]{:S(2)}) async-start(bf16[8,4,512]{2,1,0:T(4,128)(2,1)} %broadcast_in_dim.47), calls=%async_computation.2 | async-start | bytes 65536 | tf_op jit(solution)/shard_map/all_to_all | solution.py:157
  115.1 6.7 %all-to-all-done.2 = bf16[8,4,512]{2,1,0:T(4,128)(2,1)S(1)} async-done(((bf16[8,4,512]{2,1,0:T(4,128)(2,1)}), bf16[8,4,512]{2,1,0:T(4,128)(2,1)S(1)}, u32[]{:S(2)}, u32[]{:S(2)}) %all-to-all-start.2) | async-done | bytes 32800 | tf_op jit(solution)/shard_map/all_to_all | solution.py:157
  121.9 3.6 %convolution_convert_fusion.4 = bf16[512,512]{1,0:T(8,128)(2,1)S(1)} fusion(bf16[512,2048]{1,0:T(8,128)(2,1)} %get-tuple-element.12, bf16[2048,512]{1,0:T(8,128)(2,1)} %collective-permute-done.6), kind=kOutput, calls=%fused_computation.47 | convolution fusion | flops 1074003968 | bytes 4718592 | tf_op jit(solution)/shard_map/dot_general | solution.py:115
  130.4 6.2 %collective-permute-done.7 = bf16[512,512]{1,0:T(8,128)(2,1)S(1)} collective-permute-done((bf16[512,512]{1,0:T(8,128)(2,1)S(1)}, bf16[512,512]{1,0:T(8,128)(2,1)S(1)}, u32[]{:S(2)}, u32[]{:S(2)}) %collective-permute-start.7) | collective-permute-done | bytes 524320 | tf_op jit(solution)/shard_map/ppermute | solution.py:42
  136.6 4.0 %add_convert_fusion.2 = bf16[512,512]{1,0:T(8,128)(2,1)} fusion(bf16[512,512]{1,0:T(8,128)(2,1)S(1)} %collective-permute-done.7, bf16[512,2048]{1,0:T(8,128)(2,1)} %get-tuple-element.12, bf16[2048,512]{1,0:T(8,128)(2,1)S(1)} %copy-done.2, f32[512]{0:T(512)S(1)} %add_rsqrt_fusion.2, s32[]{:T(128)S(6)} %select_n.213), kind=kOutput, calls=%fused_computation.66 | convolution fusion | flops 1076887552 | bytes 5769220 | tf_op jit(solution)/shard_map/dot_general | solution.py:117
  151.4 6.0 %all_gather.15 = bf16[32,4096]{1,0:T(8,128)(2,1)S(1)} all-gather(bf16[8,4096]{1,0:T(8,128)(2,1)} %param.18), channel_id=1, replica_groups=mesh['section'=4,'dp'=8] {'section'}, dimensions={0}, use_global_device_ids=true | all-gather | bytes 327680 | tf_op jit(solution)/shard_map/all_gather | solution.py:109
  159.4 3.3 %all-to-all-start.3 = ((bf16[8,4,512]{2,1,0:T(4,128)(2,1)}), bf16[8,4,512]{2,1,0:T(4,128)(2,1)S(1)}, u32[]{:S(2)}, u32[]{:S(2)}) async-start(bf16[8,4,512]{2,1,0:T(4,128)(2,1)} %broadcast_in_dim.48), calls=%async_computation.3 | async-start | bytes 65536 | tf_op jit(solution)/shard_map/all_to_all | solution.py:157
  164.8 4.9 %all-to-all-done.3 = bf16[8,4,512]{2,1,0:T(4,128)(2,1)S(1)} async-done(((bf16[8,4,512]{2,1,0:T(4,128)(2,1)}), bf16[8,4,512]{2,1,0:T(4,128)(2,1)S(1)}, u32[]{:S(2)}, u32[]{:S(2)}) %all-to-all-start.3) | async-done | bytes 32800 | tf_op jit(solution)/shard_map/all_to_all | solution.py:157
  184.0 7.8 %collective-permute-done.15 = f32[512]{0:T(512)S(1)} collective-permute-done((f32[512]{0:T(512)S(1)}, f32[512]{0:T(512)S(1)}, u32[]{:S(2)}, u32[]{:S(2)}) %collective-permute-start.15) | collective-permute-done | bytes 2080 | tf_op jit(solution)/shard_map/ppermute | solution.py:42
  200.2 5.4 %all-gather.1 = bf16[4,12,512]{2,1,0:T(8,128)(2,1)S(1)} all-gather(bf16[1,12,512]{2,1,0:T(8,128)(2,1)S(1)} %maximum_bitcast_fusion), channel_id=2, replica_groups=mesh['section'=4,'dp'=8] {'section'}, dimensions={0}, use_global_device_ids=true | all-gather | bytes 61440 | tf_op jit(solution)/shard_map/all_gather | solution.py:178
  206.3 3.4 %all-to-all-start.4 = ((bf16[8,12,512]{2,1,0:T(8,128)(2,1)}), bf16[8,12,512]{2,1,0:T(8,128)(2,1)S(1)}, u32[]{:S(2)}, u32[]{:S(2)}) async-start(bf16[8,12,512]{2,1,0:T(8,128)(2,1)} %broadcast_in_dim.50), calls=%async_computation.4 | async-start | bytes 262144 | tf_op jit(solution)/shard_map/all_to_all | solution.py:157
  212.6 4.8 %all-to-all-done.4 = bf16[8,12,512]{2,1,0:T(8,128)(2,1)S(1)} async-done(((bf16[8,12,512]{2,1,0:T(8,128)(2,1)}), bf16[8,12,512]{2,1,0:T(8,128)(2,1)S(1)}, u32[]{:S(2)}, u32[]{:S(2)}) %all-to-all-start.4) | async-done | bytes 98336 | tf_op jit(solution)/shard_map/all_to_all | solution.py:157
  225.5 3.7 %collective-permute-start.21 = (f32[512]{0:T(512)S(1)}, f32[512]{0:T(512)S(1)}, u32[]{:S(2)}, u32[]{:S(2)}) collective-permute-start(f32[512]{0:T(512)S(1)} %get-tuple-element.7), channel_id=1, source_target_pairs={{0,1},{1,0},{2,3},{3,2},{4,5},{5,4},{6,7},{7,6},{8,9},{9,8},{10,11... | collective-permute-start | bytes 6152 | tf_op jit(solution)/shard_map/ppermute | solution.py:42
  229.5 4.6 %collective-permute-done.21 = f32[512]{0:T(512)S(1)} collective-permute-done((f32[512]{0:T(512)S(1)}, f32[512]{0:T(512)S(1)}, u32[]{:S(2)}, u32[]{:S(2)}) %collective-permute-start.21) | collective-permute-done | bytes 2080 | tf_op jit(solution)/shard_map/ppermute | solution.py:42
  237.3 3.5 %all-to-all-start = ((bf16[8,64,512]{2,1,0:T(8,128)(2,1)}), bf16[8,64,512]{2,1,0:T(8,128)(2,1)S(1)}, u32[]{:S(2)}, u32[]{:S(2)}) async-start(bf16[8,64,512]{2,1,0:T(8,128)(2,1)} %bitcast.14), calls=%async_computation | async-start | bytes 1048576 | tf_op jit(solution)/shard_map/all_to_all | solution.py:152
  242.4 31.2 %all_gather.14 = f32[32,64]{1,0:T(8,128)S(1)} all-gather(f32[8,64]{1,0:T(8,128)S(1)} %select_reduce_fusion), channel_id=1, replica_groups=mesh['section'=4,'dp'=8] {'section'}, dimensions={0}, use_global_device_ids=true | all-gather | bytes 10240 | tf_op jit(solution)/shard_map/all_gather | solution.py:209
  275.0 6.0 %all-to-all-start.5 = ((bf16[8,8,4096]{2,1,0:T(8,128)(2,1)}), bf16[8,8,4096]{2,1,0:T(8,128)(2,1)S(1)}, u32[]{:S(2)}, u32[]{:S(2)}) async-start(bf16[8,8,4096]{2,1,0:T(8,128)(2,1)} %fusion.1), calls=%async_computation.5 | async-start | bytes 1048576 | tf_op jit(solution)/shard_map/all_to_all | solution.py:214
  284.1 12.0 %all-to-all-done.5 = bf16[8,8,4096]{2,1,0:T(8,128)(2,1)S(1)} async-done(((bf16[8,8,4096]{2,1,0:T(8,128)(2,1)}), bf16[8,8,4096]{2,1,0:T(8,128)(2,1)S(1)}, u32[]{:S(2)}, u32[]{:S(2)}) %all-to-all-start.5) | async-done | bytes 524320 | tf_op jit(solution)/shard_map/all_to_all | solution.py:214
  (183 shorter events, 105.0 us)
Async XLA Ops:
  7.9 114.0 %collective-permute-start.6 = (bf16[2048,512]{1,0:T(8,128)(2,1)}, bf16[2048,512]{1,0:T(8,128)(2,1)}, u32[]{:S(2)}, u32[]{:S(2)}) collective-permute-start(bf16[2048,512]{1,0:T(8,128)(2,1)} %fusion.2), channel_id=1, source_target_pairs={{0,1},{1,0},{2,3},{3,2},{4,5},{5,4},{6,7},{7,6}} | collective-permute-start | bytes 6291464 | tf_op jit(solution)/shard_map/ppermute | solution.py:42
  12.8 161.1 %collective-permute-start.13 = (bf16[2048,512]{1,0:T(8,128)(2,1)}, bf16[2048,512]{1,0:T(8,128)(2,1)}, u32[]{:S(2)}, u32[]{:S(2)}) collective-permute-start(bf16[2048,512]{1,0:T(8,128)(2,1)} %fusion.2), channel_id=1, source_target_pairs={{8,9},{9,8},{10,11},{11,10},{12,13},{13,12},{14,15},{15,14},{16,17... | collective-permute-start | bytes 6291464 | tf_op jit(solution)/shard_map/ppermute | solution.py:42
  17.1 51.0 %collective-permute-start = (bf16[64,2048]{1,0:T(8,128)(2,1)}, bf16[64,2048]{1,0:T(8,128)(2,1)}, u32[]{:S(2)}, u32[]{:S(2)}) collective-permute-start(bf16[64,2048]{1,0:T(8,128)(2,1)} %get-tuple-element.14), channel_id=1, source_target_pairs={{0,1},{1,0},{2,3},{3,2},{4,5},{5,4},{6,7},{7,6},{16,17},{17,16},{1... | collective-permute-start | bytes 786440 | tf_op jit(solution)/shard_map/ppermute | solution.py:42
  21.9 83.0 %all-to-all-start.1 = ((bf16[8,8,4736]{2,1,0:T(8,128)(2,1)}), bf16[8,8,4736]{2,1,0:T(8,128)(2,1)S(1)}, u32[]{:S(2)}, u32[]{:S(2)}) async-start(bf16[8,8,4736]{2,1,0:T(8,128)(2,1)} %pad_maximum_fusion.1), calls=%async_computation.1 | async-start | bytes 1212416 | tf_op jit(solution)/shard_map/all_to_all | solution.py:108
  69.2 13.3 %collective-permute-start.3 = (bf16[128,2048]{1,0:T(8,128)(2,1)S(1)}, bf16[128,2048]{1,0:T(8,128)(2,1)S(1)}, u32[]{:S(2)}, u32[]{:S(2)}) collective-permute-start(bf16[128,2048]{1,0:T(8,128)(2,1)S(1)} %maximum_select_fusion.2), channel_id=1, source_target_pairs={{0,6},{1,7},{2,4},{3,5},{4,2},{5,3},{6,0},{7,1},{16,22},{17,23},{1... | collective-permute-start | bytes 1572872 | tf_op jit(solution)/shard_map/ppermute | solution.py:42
  75.3 23.4 %collective-permute-start.2 = (bf16[128,2048]{1,0:T(8,128)(2,1)S(1)}, bf16[128,2048]{1,0:T(8,128)(2,1)S(1)}, u32[]{:S(2)}, u32[]{:S(2)}) collective-permute-start(bf16[128,2048]{1,0:T(8,128)(2,1)S(1)} %maximum_select_fusion.2), channel_id=1, source_target_pairs={{0,4},{1,5},{2,6},{3,7},{4,0},{5,1},{6,2},{7,3},{16,20},{17,21},{1... | collective-permute-start | bytes 1572872 | tf_op jit(solution)/shard_map/ppermute | solution.py:42
  77.2 21.5 %collective-permute-start.1 = (bf16[128,2048]{1,0:T(8,128)(2,1)S(1)}, bf16[128,2048]{1,0:T(8,128)(2,1)S(1)}, u32[]{:S(2)}, u32[]{:S(2)}) collective-permute-start(bf16[128,2048]{1,0:T(8,128)(2,1)S(1)} %maximum_select_fusion.2), channel_id=1, source_target_pairs={{0,2},{1,3},{2,0},{3,1},{4,6},{5,7},{6,4},{7,5},{16,18},{17,19},{1... | collective-permute-start | bytes 1572872 | tf_op jit(solution)/shard_map/ppermute | solution.py:42
  100.3 49.0 %collective-permute-start.5 = (bf16[512,2048]{1,0:T(8,128)(2,1)}, bf16[512,2048]{1,0:T(8,128)(2,1)}, u32[]{:S(2)}, u32[]{:S(2)}) collective-permute-start(bf16[512,2048]{1,0:T(8,128)(2,1)} %get-tuple-element.12), channel_id=1, source_target_pairs={{16,0},{17,1},{18,2},{19,3},{20,4},{21,5},{22,6},{23,7}} | collective-permute-start | bytes 6291464 | tf_op jit(solution)/shard_map/ppermute | solution.py:42
  101.6 13.5 %collective-permute-start.8 = (f32[512]{0:T(512)S(1)}, f32[512]{0:T(512)S(1)}, u32[]{:S(2)}, u32[]{:S(2)}) collective-permute-start(f32[512]{0:T(512)S(1)} %get-tuple-element.11), channel_id=1, source_target_pairs={{0,1},{1,0},{2,3},{3,2},{4,5},{5,4},{6,7},{7,6}} | collective-permute-start | bytes 6152 | tf_op jit(solution)/shard_map/ppermute | solution.py:42
  125.6 11.1 %collective-permute-start.7 = (bf16[512,512]{1,0:T(8,128)(2,1)S(1)}, bf16[512,512]{1,0:T(8,128)(2,1)S(1)}, u32[]{:S(2)}, u32[]{:S(2)}) collective-permute-start(bf16[512,512]{1,0:T(8,128)(2,1)S(1)} %convolution_convert_fusion.4), channel_id=1, source_target_pairs={{0,1},{1,0},{2,3},{3,2},{4,5},{5,4},{6,7},{7,6}} | collective-permute-start | bytes 1572872 | tf_op jit(solution)/shard_map/ppermute | solution.py:42
  128.8 18.4 %collective-permute-start.24 = (bf16[4,512]{1,0:T(4,128)(2,1)S(1)}, bf16[4,512]{1,0:T(4,128)(2,1)S(1)}, u32[]{:S(2)}, u32[]{:S(2)}) collective-permute-start(bf16[4,512]{1,0:T(4,128)(2,1)S(1)} %fusion.67), channel_id=1, source_target_pairs={{0,8},{1,9},{2,10},{3,11},{4,12},{5,13},{6,14},{7,15},{8,16},{9,17... | collective-permute-start | bytes 12296 | tf_op jit(solution)/shard_map/ppermute | solution.py:42
  143.0 26.9 %collective-permute-start.12 = (bf16[512,512]{1,0:T(8,128)(2,1)}, bf16[512,512]{1,0:T(8,128)(2,1)}, u32[]{:S(2)}, u32[]{:S(2)}) collective-permute-start(bf16[512,512]{1,0:T(8,128)(2,1)} %bitcast.132), channel_id=1, source_target_pairs={{0,14},{1,15},{2,12},{3,13},{4,10},{5,11},{6,8},{7,9}} | collective-permute-start | bytes 1572872 | tf_op jit(solution)/shard_map/ppermute | solution.py:42
  145.1 26.1 %collective-permute-start.11 = (bf16[512,512]{1,0:T(8,128)(2,1)}, bf16[512,512]{1,0:T(8,128)(2,1)}, u32[]{:S(2)}, u32[]{:S(2)}) collective-permute-start(bf16[512,512]{1,0:T(8,128)(2,1)} %bitcast.133), channel_id=1, source_target_pairs={{0,12},{1,13},{2,14},{3,15},{4,8},{5,9},{6,10},{7,11}} | collective-permute-start | bytes 1572872 | tf_op jit(solution)/shard_map/ppermute | solution.py:42
  147.2 24.0 %collective-permute-start.10 = (bf16[512,512]{1,0:T(8,128)(2,1)}, bf16[512,512]{1,0:T(8,128)(2,1)}, u32[]{:S(2)}, u32[]{:S(2)}) collective-permute-start(bf16[512,512]{1,0:T(8,128)(2,1)} %bitcast.134), channel_id=1, source_target_pairs={{0,10},{1,11},{2,8},{3,9},{4,14},{5,15},{6,12},{7,13}} | collective-permute-start | bytes 1572872 | tf_op jit(solution)/shard_map/ppermute | solution.py:42
  149.3 21.9 %collective-permute-start.9 = (bf16[512,512]{1,0:T(8,128)(2,1)}, bf16[512,512]{1,0:T(8,128)(2,1)}, u32[]{:S(2)}, u32[]{:S(2)}) collective-permute-start(bf16[512,512]{1,0:T(8,128)(2,1)} %bitcast.135), channel_id=1, source_target_pairs={{0,8},{1,9},{2,10},{3,11},{4,12},{5,13},{6,14},{7,15}} | collective-permute-start | bytes 1572872 | tf_op jit(solution)/shard_map/ppermute | solution.py:42
  169.9 47.7 %collective-permute-start.4 = (bf16[512,2048]{1,0:T(8,128)(2,1)}, bf16[512,2048]{1,0:T(8,128)(2,1)}, u32[]{:S(2)}, u32[]{:S(2)}) collective-permute-start(bf16[512,2048]{1,0:T(8,128)(2,1)} %get-tuple-element.12), channel_id=1, source_target_pairs={{24,0},{25,1},{26,2},{27,3},{28,4},{29,5},{30,6},{31,7}} | collective-permute-start | bytes 6291464 | tf_op jit(solution)/shard_map/ppermute | solution.py:42
  176.8 15.1 %collective-permute-start.14 = (bf16[512,512]{1,0:T(8,128)(2,1)S(1)}, bf16[512,512]{1,0:T(8,128)(2,1)S(1)}, u32[]{:S(2)}, u32[]{:S(2)}) collective-permute-start(bf16[512,512]{1,0:T(8,128)(2,1)S(1)} %convolution_convert_fusion.3), channel_id=1, source_target_pairs={{0,1},{1,0},{2,3},{3,2},{4,5},{5,4},{6,7},{7,6},{8,9},{9,8},{10,11... | collective-permute-start | bytes 1572872 | tf_op jit(solution)/shard_map/ppermute | solution.py:42
  180.1 11.7 %collective-permute-start.15 = (f32[512]{0:T(512)S(1)}, f32[512]{0:T(512)S(1)}, u32[]{:S(2)}, u32[]{:S(2)}) collective-permute-start(f32[512]{0:T(512)S(1)} %get-tuple-element.9), channel_id=1, source_target_pairs={{0,1},{1,0},{2,3},{3,2},{4,5},{5,4},{6,7},{7,6},{8,9},{9,8},{10,11... | collective-permute-start | bytes 6152 | tf_op jit(solution)/shard_map/ppermute | solution.py:42
  195.9 13.8 %collective-permute-start.16 = (bf16[512,512]{1,0:T(8,128)(2,1)S(1)}, bf16[512,512]{1,0:T(8,128)(2,1)S(1)}, u32[]{:S(2)}, u32[]{:S(2)}) collective-permute-start(bf16[512,512]{1,0:T(8,128)(2,1)S(1)} %bitcast.136), channel_id=1, source_target_pairs={{0,8},{1,9},{2,10},{3,11},{4,12},{5,13},{6,14},{7,15},{8,16},{9,17... | collective-permute-start | bytes 1572872 | tf_op jit(solution)/shard_map/ppermute | solution.py:42
  206.3 11.1 %all-to-all-start.4 = ((bf16[8,12,512]{2,1,0:T(8,128)(2,1)}), bf16[8,12,512]{2,1,0:T(8,128)(2,1)S(1)}, u32[]{:S(2)}, u32[]{:S(2)}) async-start(bf16[8,12,512]{2,1,0:T(8,128)(2,1)} %broadcast_in_dim.50), calls=%async_computation.4 | async-start | bytes 262144 | tf_op jit(solution)/shard_map/all_to_all | solution.py:157
  222.9 11.2 %collective-permute-start.20 = (bf16[512,512]{1,0:T(8,128)(2,1)S(1)}, bf16[512,512]{1,0:T(8,128)(2,1)S(1)}, u32[]{:S(2)}, u32[]{:S(2)}) collective-permute-start(bf16[512,512]{1,0:T(8,128)(2,1)S(1)} %convolution_convert_fusion.2), channel_id=1, source_target_pairs={{0,1},{1,0},{2,3},{3,2},{4,5},{5,4},{6,7},{7,6},{8,9},{9,8},{10,11... | collective-permute-start | bytes 1572872 | tf_op jit(solution)/shard_map/ppermute | solution.py:42
  237.3 37.7 %all-to-all-start = ((bf16[8,64,512]{2,1,0:T(8,128)(2,1)}), bf16[8,64,512]{2,1,0:T(8,128)(2,1)S(1)}, u32[]{:S(2)}, u32[]{:S(2)}) async-start(bf16[8,64,512]{2,1,0:T(8,128)(2,1)} %bitcast.14), calls=%async_computation | async-start | bytes 1048576 | tf_op jit(solution)/shard_map/all_to_all | solution.py:152
  275.0 21.0 %all-to-all-start.5 = ((bf16[8,8,4096]{2,1,0:T(8,128)(2,1)}), bf16[8,8,4096]{2,1,0:T(8,128)(2,1)S(1)}, u32[]{:S(2)}, u32[]{:S(2)}) async-start(bf16[8,8,4096]{2,1,0:T(8,128)(2,1)} %fusion.1), calls=%async_computation.5 | async-start | bytes 1048576 | tf_op jit(solution)/shard_map/all_to_all | solution.py:214
  281.1 17.2 %collective-permute-start.22 = (bf16[64,4096]{1,0:T(8,128)(2,1)S(1)}, bf16[64,4096]{1,0:T(8,128)(2,1)S(1)}, u32[]{:S(2)}, u32[]{:S(2)}) collective-permute-start(bf16[64,4096]{1,0:T(8,128)(2,1)S(1)} %bitcast.131), channel_id=1, source_target_pairs={{0,8},{1,9},{2,10},{3,11},{4,12},{5,13},{6,14},{7,15},{8,16},{9,17... | collective-permute-start | bytes 1572872 | tf_op jit(solution)/shard_map/ppermute | solution.py:42
  (29 other events, 267.6 us)

commit v3 on v2

--- a/solution.py
+++ b/solution.py
@@ -58,7 +58,8 @@
         return wide.astype(jnp.bfloat16).reshape(inner, cols)
 
     def split_weights(order, firsts):
-        mine, theirs = gained(order, side), gained(order, 1 - side)
+        theirs = gained(order, 1 - side)
+        mine = gained(order, side)
         rest = [a for a in range(sections - 1) if a not in firsts]
         came = send(theirs, [(a, a, 1) for a in firsts])
         if rest:
@@ -112,7 +113,8 @@
         wide = states.astype(jnp.float32)
         square = jnp.sum(wide * wide, axis=-1)
         other_square = send(square, hops)
-        part = jnp.dot(states, theirs, preferred_element_type=jnp.float32).astype(jnp.bfloat16)
+        part = jnp.dot(states, theirs, preferred_element_type=jnp.float32)
+        part = part.astype(jnp.bfloat16)
         other = send(part, hops)
         own = jnp.dot(states, mine, preferred_element_type=jnp.float32)
         inv_rms = lax.rsqrt((square + other_square) / width + epsilon)
@@ -151,7 +153,7 @@
         block = reorder(block, place - flips)
     tokens = lax.all_to_all(block, "dp", split_axis=0, concat_axis=1, tiled=True)
     shifted = send(tokens, [(a, a + 1, 0) for a in range(sections - 1)])
-    held_out = jnp.where(section == 0, fresh_batches[TICKS - 1], shifted)
+    held_out = jnp.where(section == 0, fresh_batches[TICKS - 1], shifted)[None]
 
     def spread(x):
         pieces = lax.all_to_all(
@@ -212,8 +214,10 @@
     ).astype(jnp.bfloat16)
     query_grad = jnp.dot(row_grad, received_wide, precision=lax.Precision.HIGHEST)
     returned = lax.all_to_all(received_grad, "dp", split_axis=0, concat_axis=0, tiled=True)
-    pool_grad = jnp.zeros(returned.shape, jnp.bfloat16).at[route[0]].set(returned)
-    return (held_out[None], losses, query_grad, pool_grad)
+    spots = jnp.arange(rows)
+    back = jnp.sum(jnp.where(route[0][None, :] == spots[:, None], spots[None, :], 0), axis=1)
+    pool_grad = rows_at(returned, back)
+    return (held_out, losses, query_grad, pool_grad)
 
 
 def solution(mesh):

time: 302 us -> 301 us (level)
    gather x8 -> x9, local copies, waits for them, and re-layouts: 13.5 us -> 15.2 us  [rows_at(): return x.at[index].get(mode='promise_in_bounds')]
where the time goes in v3:
time: 301 us; the launch traced here: 300 us
  waiting for transfers between devices  100 us (33%)
  starting transfers between devices  83.2 us (28%)
  blocking collectives  42.7 us (14%)
  matrix products  26.5 us (9%)
  other arithmetic  23.3 us (8%)
  local copies, waits for them, and re-layouts  22.4 us (7%)
    ppermute x25, waiting for transfers between devices, send(): lax.ppermute(x, AXES, [(a * dps + i, b * dps + (i ^ flip)) for a, b, flip...  71.9 us
    ppermute x25, starting transfers between devices, send(): lax.ppermute(x, AXES, [(a * dps + i, b * dps + (i ^ flip)) for a, b, flip...  56.9 us
    all_gather x1, blocking collectives, on_device(): owner_grads = lax.all_gather(row_grad, 'section', axis=0, tiled=True)  31.3 us
    all_to_all x3, waiting for transfers between devices, spread(): lax.all_to_all(jnp.broadcast_to(x[None], (dps, *x.shape)), 'dp', split_ax...  16.3 us
    gather x9, local copies, waits for them, and re-layouts, rows_at(): return x.at[index].get(mode='promise_in_bounds')  15.2 us
    all_to_all x1, waiting for transfers between devices, on_device(): lax.all_to_all(received_grad, 'dp', split_axis=0, concat_axis=0, tiled=True)  11.8 us
    all_to_all x3, starting transfers between devices, spread(): lax.all_to_all(jnp.broadcast_to(x[None], (dps, *x.shape)), 'dp', split_ax...  10.5 us
    dot_general x3, matrix products, layer(): part = jnp.dot(states, theirs, preferred_element_type=jnp.float32)  9.41 us
  transfers between devices with their start and end apart: 31, of which 10 were waited for; matrix products, arithmetic and copies ran while one was open for 18% of the time, Pallas kernels for 0%

profile of v3, /device:TPU:0, one launch (start us, length us, event | category | flops | bytes accessed | tf_op | source)
XLA Modules:
  0.0 299.7 jit_solution(15997355940210830631)
XLA Ops:
  7.9 4.9 %collective-permute-start.6 = (bf16[2048,512]{1,0:T(8,128)(2,1)}, bf16[2048,512]{1,0:T(8,128)(2,1)}, u32[]{:S(2)}, u32[]{:S(2)}) collective-permute-start(bf16[2048,512]{1,0:T(8,128)(2,1)} %fusion.2), channel_id=1, source_target_pairs={{0,1},{1,0},{2,3},{3,2},{4,5},{5,4},{6,7},{7,6}} | collective-permute-start | bytes 6291464 | tf_op jit(solution)/shard_map/ppermute | solution.py:42
  21.9 6.3 %all-to-all-start.1 = ((bf16[8,8,4736]{2,1,0:T(8,128)(2,1)}), bf16[8,8,4736]{2,1,0:T(8,128)(2,1)S(1)}, u32[]{:S(2)}, u32[]{:S(2)}) async-start(bf16[8,8,4736]{2,1,0:T(8,128)(2,1)} %pad_maximum_fusion.1), calls=%async_computation.1 | async-start | bytes 1212416 | tf_op jit(solution)/shard_map/all_to_all | solution.py:109
  32.1 36.0 %collective-permute-done = bf16[64,2048]{1,0:T(8,128)(2,1)} collective-permute-done((bf16[64,2048]{1,0:T(8,128)(2,1)}, bf16[64,2048]{1,0:T(8,128)(2,1)}, u32[]{:S(2)}, u32[]{:S(2)}) %collective-permute-start) | collective-permute-done | bytes 262176 | tf_op jit(solution)/shard_map/ppermute | solution.py:42
  69.2 6.0 %collective-permute-start.3 = (bf16[128,2048]{1,0:T(8,128)(2,1)S(1)}, bf16[128,2048]{1,0:T(8,128)(2,1)S(1)}, u32[]{:S(2)}, u32[]{:S(2)}) collective-permute-start(bf16[128,2048]{1,0:T(8,128)(2,1)S(1)} %maximum_select_fusion.2), channel_id=1, source_target_pairs={{0,6},{1,7},{2,4},{3,5},{4,2},{5,3},{6,0},{7,1},{16,22},{17,23},{1... | collective-permute-start | bytes 1572872 | tf_op jit(solution)/shard_map/ppermute | solution.py:42
  82.5 16.2 %collective-permute-done.2 = bf16[128,2048]{1,0:T(8,128)(2,1)S(1)} collective-permute-done((bf16[128,2048]{1,0:T(8,128)(2,1)S(1)}, bf16[128,2048]{1,0:T(8,128)(2,1)S(1)}, u32[]{:S(2)}, u32[]{:S(2)}) %collective-permute-start.2) | collective-permute-done | bytes 524320 | tf_op jit(solution)/shard_map/ppermute | solution.py:42
  101.5 3.4 %collective-permute-start.8 = (f32[512]{0:T(512)S(1)}, f32[512]{0:T(512)S(1)}, u32[]{:S(2)}, u32[]{:S(2)}) collective-permute-start(f32[512]{0:T(512)S(1)} %get-tuple-element.11), channel_id=1, source_target_pairs={{0,1},{1,0},{2,3},{3,2},{4,5},{5,4},{6,7},{7,6}} | collective-permute-start | bytes 6152 | tf_op jit(solution)/shard_map/ppermute | solution.py:42
  111.3 3.8 %all-to-all-start.2 = ((bf16[8,4,512]{2,1,0:T(4,128)(2,1)}), bf16[8,4,512]{2,1,0:T(4,128)(2,1)S(1)}, u32[]{:S(2)}, u32[]{:S(2)}) async-start(bf16[8,4,512]{2,1,0:T(4,128)(2,1)} %broadcast_in_dim.57), calls=%async_computation.2 | async-start | bytes 65536 | tf_op jit(solution)/shard_map/all_to_all | solution.py:159
  115.0 6.7 %all-to-all-done.2 = bf16[8,4,512]{2,1,0:T(4,128)(2,1)S(1)} async-done(((bf16[8,4,512]{2,1,0:T(4,128)(2,1)}), bf16[8,4,512]{2,1,0:T(4,128)(2,1)S(1)}, u32[]{:S(2)}, u32[]{:S(2)}) %all-to-all-start.2) | async-done | bytes 32800 | tf_op jit(solution)/shard_map/all_to_all | solution.py:159
  121.9 3.6 %convolution_convert_fusion.4 = bf16[512,512]{1,0:T(8,128)(2,1)S(1)} fusion(bf16[512,2048]{1,0:T(8,128)(2,1)} %get-tuple-element.12, bf16[2048,512]{1,0:T(8,128)(2,1)} %collective-permute-done.6), kind=kOutput, calls=%fused_computation.47 | convolution fusion | flops 1074003968 | bytes 4718592 | tf_op jit(solution)/shard_map/dot_general | solution.py:116
  130.4 6.2 %collective-permute-done.7 = bf16[512,512]{1,0:T(8,128)(2,1)S(1)} collective-permute-done((bf16[512,512]{1,0:T(8,128)(2,1)S(1)}, bf16[512,512]{1,0:T(8,128)(2,1)S(1)}, u32[]{:S(2)}, u32[]{:S(2)}) %collective-permute-start.7) | collective-permute-done | bytes 524320 | tf_op jit(solution)/shard_map/ppermute | solution.py:42
  136.6 4.0 %add_convert_fusion.2 = bf16[512,512]{1,0:T(8,128)(2,1)} fusion(bf16[512,512]{1,0:T(8,128)(2,1)S(1)} %collective-permute-done.7, bf16[512,2048]{1,0:T(8,128)(2,1)} %get-tuple-element.12, bf16[2048,512]{1,0:T(8,128)(2,1)S(1)} %copy-done.2, f32[512]{0:T(512)S(1)} %add_rsqrt_fusion.2, s32[]{:T(128)S(6)} %select_n.226), kind=kOutput, calls=%fused_computation.66 | convolution fusion | flops 1076887552 | bytes 5769220 | tf_op jit(solution)/shard_map/dot_general | solution.py:119
  151.4 6.0 %all_gather.15 = bf16[32,4096]{1,0:T(8,128)(2,1)S(1)} all-gather(bf16[8,4096]{1,0:T(8,128)(2,1)} %param.18), channel_id=1, replica_groups=mesh['section'=4,'dp'=8] {'section'}, dimensions={0}, use_global_device_ids=true | all-gather | bytes 327680 | tf_op jit(solution)/shard_map/all_gather | solution.py:110
  159.4 3.3 %all-to-all-start.3 = ((bf16[8,4,512]{2,1,0:T(4,128)(2,1)}), bf16[8,4,512]{2,1,0:T(4,128)(2,1)S(1)}, u32[]{:S(2)}, u32[]{:S(2)}) async-start(bf16[8,4,512]{2,1,0:T(4,128)(2,1)} %broadcast_in_dim.60), calls=%async_computation.3 | async-start | bytes 65536 | tf_op jit(solution)/shard_map/all_to_all | solution.py:159
  164.9 4.8 %all-to-all-done.3 = bf16[8,4,512]{2,1,0:T(4,128)(2,1)S(1)} async-done(((bf16[8,4,512]{2,1,0:T(4,128)(2,1)}), bf16[8,4,512]{2,1,0:T(4,128)(2,1)S(1)}, u32[]{:S(2)}, u32[]{:S(2)}) %all-to-all-start.3) | async-done | bytes 32800 | tf_op jit(solution)/shard_map/all_to_all | solution.py:159
  183.9 7.9 %collective-permute-done.15 = f32[512]{0:T(512)S(1)} collective-permute-done((f32[512]{0:T(512)S(1)}, f32[512]{0:T(512)S(1)}, u32[]{:S(2)}, u32[]{:S(2)}) %collective-permute-start.15) | collective-permute-done | bytes 2080 | tf_op jit(solution)/shard_map/ppermute | solution.py:42
  200.2 5.4 %all-gather.1 = bf16[4,12,512]{2,1,0:T(8,128)(2,1)S(1)} all-gather(bf16[1,12,512]{2,1,0:T(8,128)(2,1)S(1)} %maximum_bitcast_fusion), channel_id=2, replica_groups=mesh['section'=4,'dp'=8] {'section'}, dimensions={0}, use_global_device_ids=true | all-gather | bytes 61440 | tf_op jit(solution)/shard_map/all_gather | solution.py:180
  206.3 3.4 %all-to-all-start.4 = ((bf16[8,12,512]{2,1,0:T(8,128)(2,1)}), bf16[8,12,512]{2,1,0:T(8,128)(2,1)S(1)}, u32[]{:S(2)}, u32[]{:S(2)}) async-start(bf16[8,12,512]{2,1,0:T(8,128)(2,1)} %broadcast_in_dim.62), calls=%async_computation.4 | async-start | bytes 262144 | tf_op jit(solution)/shard_map/all_to_all | solution.py:159
  212.6 4.8 %all-to-all-done.4 = bf16[8,12,512]{2,1,0:T(8,128)(2,1)S(1)} async-done(((bf16[8,12,512]{2,1,0:T(8,128)(2,1)}), bf16[8,12,512]{2,1,0:T(8,128)(2,1)S(1)}, u32[]{:S(2)}, u32[]{:S(2)}) %all-to-all-start.4) | async-done | bytes 98336 | tf_op jit(solution)/shard_map/all_to_all | solution.py:159
  225.5 3.7 %collective-permute-start.21 = (f32[512]{0:T(512)S(1)}, f32[512]{0:T(512)S(1)}, u32[]{:S(2)}, u32[]{:S(2)}) collective-permute-start(f32[512]{0:T(512)S(1)} %get-tuple-element.7), channel_id=1, source_target_pairs={{0,1},{1,0},{2,3},{3,2},{4,5},{5,4},{6,7},{7,6},{8,9},{9,8},{10,11... | collective-permute-start | bytes 6152 | tf_op jit(solution)/shard_map/ppermute | solution.py:42
  229.5 4.6 %collective-permute-done.21 = f32[512]{0:T(512)S(1)} collective-permute-done((f32[512]{0:T(512)S(1)}, f32[512]{0:T(512)S(1)}, u32[]{:S(2)}, u32[]{:S(2)}) %collective-permute-start.21) | collective-permute-done | bytes 2080 | tf_op jit(solution)/shard_map/ppermute | solution.py:42
  237.3 3.5 %all-to-all-start = ((bf16[8,64,512]{2,1,0:T(8,128)(2,1)}), bf16[8,64,512]{2,1,0:T(8,128)(2,1)S(1)}, u32[]{:S(2)}, u32[]{:S(2)}) async-start(bf16[8,64,512]{2,1,0:T(8,128)(2,1)} %bitcast.14), calls=%async_computation | async-start | bytes 1048576 | tf_op jit(solution)/shard_map/all_to_all | solution.py:154
  242.4 31.3 %all_gather.14 = f32[32,64]{1,0:T(8,128)S(1)} all-gather(f32[8,64]{1,0:T(8,128)S(1)} %select_reduce_fusion), channel_id=1, replica_groups=mesh['section'=4,'dp'=8] {'section'}, dimensions={0}, use_global_device_ids=true | all-gather | bytes 10240 | tf_op jit(solution)/shard_map/all_gather | solution.py:211
  275.1 6.0 %all-to-all-start.5 = ((bf16[8,8,4096]{2,1,0:T(8,128)(2,1)}), bf16[8,8,4096]{2,1,0:T(8,128)(2,1)S(1)}, u32[]{:S(2)}, u32[]{:S(2)}) async-start(bf16[8,8,4096]{2,1,0:T(8,128)(2,1)} %fusion.1), calls=%async_computation.5 | async-start | bytes 1048576 | tf_op jit(solution)/shard_map/all_to_all | solution.py:216
  284.3 11.8 %all-to-all-done.5 = bf16[8,8,4096]{2,1,0:T(8,128)(2,1)S(1)} async-done(((bf16[8,8,4096]{2,1,0:T(8,128)(2,1)}), bf16[8,8,4096]{2,1,0:T(8,128)(2,1)S(1)}, u32[]{:S(2)}, u32[]{:S(2)}) %all-to-all-start.5) | async-done | bytes 524320 | tf_op jit(solution)/shard_map/all_to_all | solution.py:216
  (186 shorter events, 104.7 us)
Async XLA Ops:
  7.9 114.0 %collective-permute-start.6 = (bf16[2048,512]{1,0:T(8,128)(2,1)}, bf16[2048,512]{1,0:T(8,128)(2,1)}, u32[]{:S(2)}, u32[]{:S(2)}) collective-permute-start(bf16[2048,512]{1,0:T(8,128)(2,1)} %fusion.2), channel_id=1, source_target_pairs={{0,1},{1,0},{2,3},{3,2},{4,5},{5,4},{6,7},{7,6}} | collective-permute-start | bytes 6291464 | tf_op jit(solution)/shard_map/ppermute | solution.py:42
  12.8 161.0 %collective-permute-start.13 = (bf16[2048,512]{1,0:T(8,128)(2,1)}, bf16[2048,512]{1,0:T(8,128)(2,1)}, u32[]{:S(2)}, u32[]{:S(2)}) collective-permute-start(bf16[2048,512]{1,0:T(8,128)(2,1)} %fusion.2), channel_id=1, source_target_pairs={{8,9},{9,8},{10,11},{11,10},{12,13},{13,12},{14,15},{15,14},{16,17... | collective-permute-start | bytes 6291464 | tf_op jit(solution)/shard_map/ppermute | solution.py:42
  17.1 51.0 %collective-permute-start = (bf16[64,2048]{1,0:T(8,128)(2,1)}, bf16[64,2048]{1,0:T(8,128)(2,1)}, u32[]{:S(2)}, u32[]{:S(2)}) collective-permute-start(bf16[64,2048]{1,0:T(8,128)(2,1)} %get-tuple-element.14), channel_id=1, source_target_pairs={{0,1},{1,0},{2,3},{3,2},{4,5},{5,4},{6,7},{7,6},{16,17},{17,16},{1... | collective-permute-start | bytes 786440 | tf_op jit(solution)/shard_map/ppermute | solution.py:42
  21.9 83.0 %all-to-all-start.1 = ((bf16[8,8,4736]{2,1,0:T(8,128)(2,1)}), bf16[8,8,4736]{2,1,0:T(8,128)(2,1)S(1)}, u32[]{:S(2)}, u32[]{:S(2)}) async-start(bf16[8,8,4736]{2,1,0:T(8,128)(2,1)} %pad_maximum_fusion.1), calls=%async_computation.1 | async-start | bytes 1212416 | tf_op jit(solution)/shard_map/all_to_all | solution.py:109
  69.2 13.3 %collective-permute-start.3 = (bf16[128,2048]{1,0:T(8,128)(2,1)S(1)}, bf16[128,2048]{1,0:T(8,128)(2,1)S(1)}, u32[]{:S(2)}, u32[]{:S(2)}) collective-permute-start(bf16[128,2048]{1,0:T(8,128)(2,1)S(1)} %maximum_select_fusion.2), channel_id=1, source_target_pairs={{0,6},{1,7},{2,4},{3,5},{4,2},{5,3},{6,0},{7,1},{16,22},{17,23},{1... | collective-permute-start | bytes 1572872 | tf_op jit(solution)/shard_map/ppermute | solution.py:42
  75.3 23.4 %collective-permute-start.2 = (bf16[128,2048]{1,0:T(8,128)(2,1)S(1)}, bf16[128,2048]{1,0:T(8,128)(2,1)S(1)}, u32[]{:S(2)}, u32[]{:S(2)}) collective-permute-start(bf16[128,2048]{1,0:T(8,128)(2,1)S(1)} %maximum_select_fusion.2), channel_id=1, source_target_pairs={{0,4},{1,5},{2,6},{3,7},{4,0},{5,1},{6,2},{7,3},{16,20},{17,21},{1... | collective-permute-start | bytes 1572872 | tf_op jit(solution)/shard_map/ppermute | solution.py:42
  77.2 21.5 %collective-permute-start.1 = (bf16[128,2048]{1,0:T(8,128)(2,1)S(1)}, bf16[128,2048]{1,0:T(8,128)(2,1)S(1)}, u32[]{:S(2)}, u32[]{:S(2)}) collective-permute-start(bf16[128,2048]{1,0:T(8,128)(2,1)S(1)} %maximum_select_fusion.2), channel_id=1, source_target_pairs={{0,2},{1,3},{2,0},{3,1},{4,6},{5,7},{6,4},{7,5},{16,18},{17,19},{1... | collective-permute-start | bytes 1572872 | tf_op jit(solution)/shard_map/ppermute | solution.py:42
  100.2 49.0 %collective-permute-start.5 = (bf16[512,2048]{1,0:T(8,128)(2,1)}, bf16[512,2048]{1,0:T(8,128)(2,1)}, u32[]{:S(2)}, u32[]{:S(2)}) collective-permute-start(bf16[512,2048]{1,0:T(8,128)(2,1)} %get-tuple-element.12), channel_id=1, source_target_pairs={{16,0},{17,1},{18,2},{19,3},{20,4},{21,5},{22,6},{23,7}} | collective-permute-start | bytes 6291464 | tf_op jit(solution)/shard_map/ppermute | solution.py:42
  101.5 13.5 %collective-permute-start.8 = (f32[512]{0:T(512)S(1)}, f32[512]{0:T(512)S(1)}, u32[]{:S(2)}, u32[]{:S(2)}) collective-permute-start(f32[512]{0:T(512)S(1)} %get-tuple-element.11), channel_id=1, source_target_pairs={{0,1},{1,0},{2,3},{3,2},{4,5},{5,4},{6,7},{7,6}} | collective-permute-start | bytes 6152 | tf_op jit(solution)/shard_map/ppermute | solution.py:42
  125.5 11.1 %collective-permute-start.7 = (bf16[512,512]{1,0:T(8,128)(2,1)S(1)}, bf16[512,512]{1,0:T(8,128)(2,1)S(1)}, u32[]{:S(2)}, u32[]{:S(2)}) collective-permute-start(bf16[512,512]{1,0:T(8,128)(2,1)S(1)} %convolution_convert_fusion.4), channel_id=1, source_target_pairs={{0,1},{1,0},{2,3},{3,2},{4,5},{5,4},{6,7},{7,6}} | collective-permute-start | bytes 1572872 | tf_op jit(solution)/shard_map/ppermute | solution.py:42
  128.7 18.5 %collective-permute-start.24 = (bf16[4,512]{1,0:T(4,128)(2,1)S(1)}, bf16[4,512]{1,0:T(4,128)(2,1)S(1)}, u32[]{:S(2)}, u32[]{:S(2)}) collective-permute-start(bf16[4,512]{1,0:T(4,128)(2,1)S(1)} %fusion.64), channel_id=1, source_target_pairs={{0,8},{1,9},{2,10},{3,11},{4,12},{5,13},{6,14},{7,15},{8,16},{9,17... | collective-permute-start | bytes 12296 | tf_op jit(solution)/shard_map/ppermute | solution.py:42
  143.0 26.9 %collective-permute-start.12 = (bf16[512,512]{1,0:T(8,128)(2,1)}, bf16[512,512]{1,0:T(8,128)(2,1)}, u32[]{:S(2)}, u32[]{:S(2)}) collective-permute-start(bf16[512,512]{1,0:T(8,128)(2,1)} %bitcast.136), channel_id=1, source_target_pairs={{0,14},{1,15},{2,12},{3,13},{4,10},{5,11},{6,8},{7,9}} | collective-permute-start | bytes 1572872 | tf_op jit(solution)/shard_map/ppermute | solution.py:42
  145.1 26.1 %collective-permute-start.11 = (bf16[512,512]{1,0:T(8,128)(2,1)}, bf16[512,512]{1,0:T(8,128)(2,1)}, u32[]{:S(2)}, u32[]{:S(2)}) collective-permute-start(bf16[512,512]{1,0:T(8,128)(2,1)} %bitcast.137), channel_id=1, source_target_pairs={{0,12},{1,13},{2,14},{3,15},{4,8},{5,9},{6,10},{7,11}} | collective-permute-start | bytes 1572872 | tf_op jit(solution)/shard_map/ppermute | solution.py:42
  147.2 24.0 %collective-permute-start.10 = (bf16[512,512]{1,0:T(8,128)(2,1)}, bf16[512,512]{1,0:T(8,128)(2,1)}, u32[]{:S(2)}, u32[]{:S(2)}) collective-permute-start(bf16[512,512]{1,0:T(8,128)(2,1)} %bitcast.138), channel_id=1, source_target_pairs={{0,10},{1,11},{2,8},{3,9},{4,14},{5,15},{6,12},{7,13}} | collective-permute-start | bytes 1572872 | tf_op jit(solution)/shard_map/ppermute | solution.py:42
  149.3 21.9 %collective-permute-start.9 = (bf16[512,512]{1,0:T(8,128)(2,1)}, bf16[512,512]{1,0:T(8,128)(2,1)}, u32[]{:S(2)}, u32[]{:S(2)}) collective-permute-start(bf16[512,512]{1,0:T(8,128)(2,1)} %bitcast.139), channel_id=1, source_target_pairs={{0,8},{1,9},{2,10},{3,11},{4,12},{5,13},{6,14},{7,15}} | collective-permute-start | bytes 1572872 | tf_op jit(solution)/shard_map/ppermute | solution.py:42
  169.8 47.8 %collective-permute-start.4 = (bf16[512,2048]{1,0:T(8,128)(2,1)}, bf16[512,2048]{1,0:T(8,128)(2,1)}, u32[]{:S(2)}, u32[]{:S(2)}) collective-permute-start(bf16[512,2048]{1,0:T(8,128)(2,1)} %get-tuple-element.12), channel_id=1, source_target_pairs={{24,0},{25,1},{26,2},{27,3},{28,4},{29,5},{30,6},{31,7}} | collective-permute-start | bytes 6291464 | tf_op jit(solution)/shard_map/ppermute | solution.py:42
  176.7 15.1 %collective-permute-start.14 = (bf16[512,512]{1,0:T(8,128)(2,1)S(1)}, bf16[512,512]{1,0:T(8,128)(2,1)S(1)}, u32[]{:S(2)}, u32[]{:S(2)}) collective-permute-start(bf16[512,512]{1,0:T(8,128)(2,1)S(1)} %convolution_convert_fusion.3), channel_id=1, source_target_pairs={{0,1},{1,0},{2,3},{3,2},{4,5},{5,4},{6,7},{7,6},{8,9},{9,8},{10,11... | collective-permute-start | bytes 1572872 | tf_op jit(solution)/shard_map/ppermute | solution.py:42
  180.1 11.8 %collective-permute-start.15 = (f32[512]{0:T(512)S(1)}, f32[512]{0:T(512)S(1)}, u32[]{:S(2)}, u32[]{:S(2)}) collective-permute-start(f32[512]{0:T(512)S(1)} %get-tuple-element.9), channel_id=1, source_target_pairs={{0,1},{1,0},{2,3},{3,2},{4,5},{5,4},{6,7},{7,6},{8,9},{9,8},{10,11... | collective-permute-start | bytes 6152 | tf_op jit(solution)/shard_map/ppermute | solution.py:42
  195.9 13.8 %collective-permute-start.16 = (bf16[512,512]{1,0:T(8,128)(2,1)S(1)}, bf16[512,512]{1,0:T(8,128)(2,1)S(1)}, u32[]{:S(2)}, u32[]{:S(2)}) collective-permute-start(bf16[512,512]{1,0:T(8,128)(2,1)S(1)} %bitcast.140), channel_id=1, source_target_pairs={{0,8},{1,9},{2,10},{3,11},{4,12},{5,13},{6,14},{7,15},{8,16},{9,17... | collective-permute-start | bytes 1572872 | tf_op jit(solution)/shard_map/ppermute | solution.py:42
  206.3 11.1 %all-to-all-start.4 = ((bf16[8,12,512]{2,1,0:T(8,128)(2,1)}), bf16[8,12,512]{2,1,0:T(8,128)(2,1)S(1)}, u32[]{:S(2)}, u32[]{:S(2)}) async-start(bf16[8,12,512]{2,1,0:T(8,128)(2,1)} %broadcast_in_dim.62), calls=%async_computation.4 | async-start | bytes 262144 | tf_op jit(solution)/shard_map/all_to_all | solution.py:159
  222.9 11.2 %collective-permute-start.20 = (bf16[512,512]{1,0:T(8,128)(2,1)S(1)}, bf16[512,512]{1,0:T(8,128)(2,1)S(1)}, u32[]{:S(2)}, u32[]{:S(2)}) collective-permute-start(bf16[512,512]{1,0:T(8,128)(2,1)S(1)} %convolution_convert_fusion.2), channel_id=1, source_target_pairs={{0,1},{1,0},{2,3},{3,2},{4,5},{5,4},{6,7},{7,6},{8,9},{9,8},{10,11... | collective-permute-start | bytes 1572872 | tf_op jit(solution)/shard_map/ppermute | solution.py:42
  237.3 37.8 %all-to-all-start = ((bf16[8,64,512]{2,1,0:T(8,128)(2,1)}), bf16[8,64,512]{2,1,0:T(8,128)(2,1)S(1)}, u32[]{:S(2)}, u32[]{:S(2)}) async-start(bf16[8,64,512]{2,1,0:T(8,128)(2,1)} %bitcast.14), calls=%async_computation | async-start | bytes 1048576 | tf_op jit(solution)/shard_map/all_to_all | solution.py:154
  275.1 21.0 %all-to-all-start.5 = ((bf16[8,8,4096]{2,1,0:T(8,128)(2,1)}), bf16[8,8,4096]{2,1,0:T(8,128)(2,1)S(1)}, u32[]{:S(2)}, u32[]{:S(2)}) async-start(bf16[8,8,4096]{2,1,0:T(8,128)(2,1)} %fusion.1), calls=%async_computation.5 | async-start | bytes 1048576 | tf_op jit(solution)/shard_map/all_to_all | solution.py:216
  281.3 16.5 %collective-permute-start.22 = (bf16[64,4096]{1,0:T(8,128)(2,1)S(1)}, bf16[64,4096]{1,0:T(8,128)(2,1)S(1)}, u32[]{:S(2)}, u32[]{:S(2)}) collective-permute-start(bf16[64,4096]{1,0:T(8,128)(2,1)S(1)} %bitcast.135), channel_id=1, source_target_pairs={{0,8},{1,9},{2,10},{3,11},{4,12},{5,13},{6,14},{7,15},{8,16},{9,17... | collective-permute-start | bytes 1572872 | tf_op jit(solution)/shard_map/ppermute | solution.py:42
  (29 other events, 312.0 us)

commit v4 on v3

--- a/solution.py
+++ b/solution.py
@@ -1,6 +1,10 @@
+import functools
+
 import jax
 import jax.numpy as jnp
 from jax import lax
+from jax.experimental import pallas as pl
+from jax.experimental.pallas import tpu as pltpu
 from jax.sharding import PartitionSpec as P
 
 
@@ -12,6 +16,141 @@
 logit_scale = 20.0
 
 AXES = ("section", "dp")
+
+
+LANES = 128
+
+
+def gain_kernel(at_ref, weight_ref, gain_ref, out_ref):
+    cols = gain_ref.shape[-1]
+    column = jnp.transpose(jnp.broadcast_to(gain_ref[0], (LANES, cols)))[:, :1]
+    out_ref[...] = (weight_ref[...].astype(jnp.float32) * column).astype(jnp.bfloat16)
+
+
+def gained_blocks(weight, gain, at):
+    cols = weight.shape[1]
+    count = at.shape[0]
+    return pl.pallas_call(
+        gain_kernel,
+        out_shape=jax.ShapeDtypeStruct((count * cols, cols), jnp.bfloat16),
+        grid_spec=pltpu.PrefetchScalarGridSpec(
+            num_scalar_prefetch=1,
+            grid=(count,),
+            in_specs=[
+                pl.BlockSpec((cols, cols), lambda k, at: (at[k], 0)),
+                pl.BlockSpec((1, 1, cols), lambda k, at: (at[k], 0, 0)),
+            ],
+            out_specs=pl.BlockSpec((cols, cols), lambda k, at: (k, 0)),
+        ),
+        cost_estimate=pl.CostEstimate(
+            flops=count * cols * cols, bytes_accessed=4 * count * cols * cols, transcendentals=0
+        ),
+    )(at, weight, gain.reshape(-1, 1, cols))
+
+
+def pick(where_ref, refs, cols):
+    *piles, wide = refs
+    for k in range(wide.shape[1] // cols):
+        block = wide[:, k * cols : (k + 1) * cols]
+        yield k, jnp.where(where_ref[0] == 1, block, piles[k][...]) if piles else block
+
+
+def sent_kernel(where_ref, *refs):
+    *states, weight_ref, out_ref, square_ref = refs
+    tile, cols = out_ref.shape[0], weight_ref.shape[1]
+    total = jnp.zeros((tile, cols), jnp.float32)
+    square = jnp.zeros((tile, 1), jnp.float32)
+    for k, block in pick(where_ref, states, cols):
+        total += jnp.dot(
+            block, weight_ref[k * cols : (k + 1) * cols, :], preferred_element_type=jnp.float32
+        )
+        wide = block.astype(jnp.float32)
+        square += jnp.sum(wide * wide, axis=-1, keepdims=True)
+    out_ref[:, :cols] = total.astype(jnp.bfloat16)
+    high = square.astype(jnp.bfloat16).astype(jnp.float32)
+    middle = (square - high).astype(jnp.bfloat16).astype(jnp.float32)
+    low = square - high - middle
+    lane = lax.broadcasted_iota(jnp.int32, (tile, LANES), 1)
+    terms = jnp.where(lane == 0, high, jnp.where(lane == 1, middle, jnp.where(lane == 2, low, 0.0)))
+    out_ref[:, cols:] = terms.astype(jnp.bfloat16)
+    square_ref[...] = jnp.broadcast_to(square, (tile, LANES))
+
+
+def kept_kernel(width, where_ref, *refs):
+    *states, weight_ref, other_ref, square_ref, wide_ref, out_ref = refs
+    _, cols = out_ref.shape
+    total = other_ref[:, :cols].astype(jnp.float32)
+    for k, block in pick(where_ref, states, cols):
+        total += jnp.dot(
+            block, weight_ref[k * cols : (k + 1) * cols, :], preferred_element_type=jnp.float32
+        )
+    square = square_ref[:, :1] + jnp.sum(
+        other_ref[:, cols:].astype(jnp.float32), axis=-1, keepdims=True
+    )
+    projected = (total * lax.rsqrt(square / width + epsilon)).astype(jnp.bfloat16)
+    kept = wide_ref[...]
+    if len(states) > 1:
+        kept = jnp.where(where_ref[0] == 1, kept, states[0][...])
+    out_ref[...] = (
+        kept.astype(jnp.float32) + jax.nn.silu(projected.astype(jnp.float32))
+    ).astype(jnp.bfloat16)
+
+
+def state_specs(states, tile):
+    return [pl.BlockSpec((tile, x.shape[1]), lambda i, at: (i, 0)) for x in states]
+
+
+def sent_half(at, states, weight, tile):
+    tokens = states[0].shape[0]
+    inner, cols = weight.shape
+    return pl.pallas_call(
+        sent_kernel,
+        out_shape=(
+            jax.ShapeDtypeStruct((tokens, cols + LANES), jnp.bfloat16),
+            jax.ShapeDtypeStruct((tokens, LANES), jnp.float32),
+        ),
+        grid_spec=pltpu.PrefetchScalarGridSpec(
+            num_scalar_prefetch=1,
+            grid=(tokens // tile,),
+            in_specs=state_specs(states, tile)
+            + [pl.BlockSpec((inner, cols), lambda i, at: (0, 0))],
+            out_specs=(
+                pl.BlockSpec((tile, cols + LANES), lambda i, at: (i, 0)),
+                pl.BlockSpec((tile, LANES), lambda i, at: (i, 0)),
+            ),
+        ),
+        cost_estimate=pl.CostEstimate(
+            flops=2 * tokens * inner * cols,
+            bytes_accessed=2 * inner * (tokens + cols),
+            transcendentals=0,
+        ),
+    )(at, *states, weight)
+
+
+def kept_half(at, states, weight, other, square, width, tile):
+    tokens = states[0].shape[0]
+    inner, cols = weight.shape
+    return pl.pallas_call(
+        functools.partial(kept_kernel, width),
+        out_shape=jax.ShapeDtypeStruct((tokens, cols), jnp.bfloat16),
+        grid_spec=pltpu.PrefetchScalarGridSpec(
+            num_scalar_prefetch=1,
+            grid=(tokens // tile,),
+            in_specs=state_specs(states, tile)
+            + [
+                pl.BlockSpec((inner, cols), lambda i, at: (0, 0)),
+                pl.BlockSpec((tile, cols + LANES), lambda i, at: (i, 0)),
+                pl.BlockSpec((tile, LANES), lambda i, at: (i, 0)),
+                pl.BlockSpec((tile, cols), lambda i, at: (i, at[1])),
+            ],
+            out_specs=pl.BlockSpec((tile, cols), lambda i, at: (i ^ at[2], 0)),
+        ),
+        cost_estimate=pl.CostEstimate(
+            flops=2 * tokens * inner * cols,
+            bytes_accessed=2 * inner * (tokens + cols),
+            transcendentals=tokens * cols,
+        ),
+    )(at, *states, weight, other, square, states[-1])
 
 
 def on_device(
@@ -46,20 +185,12 @@
     def rows_at(x, index):
         return x.at[index].get(mode="promise_in_bounds")
 
-    by_block = weight.reshape(dps, cols, cols)
-    gain_block = gain.reshape(dps, cols, 1)
     flips = jnp.where(section == 0, 0, place)
-    inner = half * cols
     last_full = sections - 1 - TICKS
 
-    def gained(order, at):
-        index = 2 * order + at
-        wide = rows_at(by_block, index).astype(jnp.float32) * rows_at(gain_block, index)
-        return wide.astype(jnp.bfloat16).reshape(inner, cols)
-
     def split_weights(order, firsts):
-        theirs = gained(order, 1 - side)
-        mine = gained(order, side)
+        theirs = gained_blocks(weight, gain, 2 * order + 1 - side)
+        mine = gained_blocks(weight, gain, 2 * order + side)
         rest = [a for a in range(sections - 1) if a not in firsts]
         came = send(theirs, [(a, a, 1) for a in firsts])
         if rest:
@@ -109,30 +240,23 @@
     inbox = lax.all_to_all(outbox, "dp", split_axis=0, concat_axis=0)
     owner_queries = lax.all_gather(queries, "section", axis=0, tiled=True)
 
-    def layer(states, mine, theirs, own_at, hops):
-        wide = states.astype(jnp.float32)
-        square = jnp.sum(wide * wide, axis=-1)
-        other_square = send(square, hops)
-        part = jnp.dot(states, theirs, preferred_element_type=jnp.float32)
-        part = part.astype(jnp.bfloat16)
+    def layer(states, mine, theirs, at, hops):
+        at = jnp.stack([jnp.asarray(x, jnp.int32) for x in at])
+        part, square = sent_half(at, states, theirs, pair_rows)
         other = send(part, hops)
-        own = jnp.dot(states, mine, preferred_element_type=jnp.float32)
-        inv_rms = lax.rsqrt((square + other_square) / width + epsilon)
-        projected = ((own + other.astype(jnp.float32)) * inv_rms[:, None]).astype(jnp.bfloat16)
-        kept = lax.dynamic_slice_in_dim(states, own_at * cols, cols, axis=1).astype(jnp.float32)
-        return (kept + jax.nn.silu(projected.astype(jnp.float32))).astype(jnp.bfloat16)
-
-    def reorder(block, flip):
-        piled = block.reshape(half, pair_rows, cols)
-        return rows_at(piled, jnp.arange(half) ^ flip).reshape(block.shape)
+        return kept_half(at, states, mine, other, square, width, pair_rows)
 
     fresh_states = []
     for i in range(TICKS - 1):
         fresh_states.append(send(states, [(sections - TICKS + 1 + i, 0, 0)]))
     block = layer(
-        states, mine_first, theirs_first, place, [(a, a, 1) for a in range(last_full + 1)]
-    )
-    block = reorder(block, place)
+        [states],
+        mine_first,
+        theirs_first,
+        (1, place, place),
+        [(a, a, 1) for a in range(last_full + 1)],
+    )
+    first = section == 0
     for tick in range(1, TICKS):
         top = last_full + tick
         if tick == 1:
@@ -146,11 +270,13 @@
                 send(block, [(a, a, 2 * k) for a in range(1, top + 1)])
                 for k in range(1, half)
             ]
-        states = jnp.where(section == 0, fresh_states[tick - 1], jnp.concatenate(piles, axis=1))
         block = layer(
-            states, mine_late, theirs_late, place - flips, [(a, a, 1) for a in range(top + 1)]
-        )
-        block = reorder(block, place - flips)
+            piles + [fresh_states[tick - 1]],
+            mine_late,
+            theirs_late,
+            (first, place, jnp.where(first, place, 0)),
+            [(a, a, 1) for a in range(top + 1)],
+        )
     tokens = lax.all_to_all(block, "dp", split_axis=0, concat_axis=1, tiled=True)
     shifted = send(tokens, [(a, a + 1, 0) for a in range(sections - 1)])
     held_out = jnp.where(section == 0, fresh_batches[TICKS - 1], shifted)[None]
@@ -174,7 +300,9 @@
         piece = (kept + jax.nn.silu(projected)).astype(jnp.bfloat16)
         exits.append(piece)
         if tick < TICKS - 1:
-            piece = send(piece, [(a, a + 1, 0) for a in range(sections - 1)])
+            piece = send(
+                piece, [(a, a + 1, 0) for a in range(sections - TICKS + tick, sections - 1)]
+            )
             ends = spread(piece)
     passages = ends.shape[0]
     exit_pieces = lax.all_gather(jnp.concatenate(exits, axis=0), "section", axis=0)

time: 301 us -> 284 us (0.944)
  waiting for transfers between devices: 100 us -> 49.7 us
  Pallas kernels: 0 us -> 48.2 us
  matrix products: 26.5 us -> 11.6 us
  local copies, waits for them, and re-layouts: 22.4 us -> 11 us
  blocking collectives: 42.7 us -> 51.9 us
  starting transfers between devices: 83.2 us -> 91 us
  other arithmetic: 23.3 us -> 17.7 us
    pallas_call x0 -> x8, Pallas kernels: none -> 48.2 us  [the longest x3 20 us: kept_half(): pl.pallas_call(functools.partial(kept_kernel, width), out_shape=jax.Shape...]
    ppermute x25 -> x22, waiting for transfers between devices: 71.9 us -> 31.5 us  [send(): lax.ppermute(x, AXES, [(a * dps + i, b * dps + (i ^ flip)) for a, b, flip...]
    all_gather x1, blocking collectives: 5.97 us -> 26.1 us  [on_device(): owner_queries = lax.all_gather(queries, 'section', axis=0, tiled=True)]
    all_gather x1, blocking collectives: 31.3 us -> 11.8 us  [on_device(): owner_grads = lax.all_gather(row_grad, 'section', axis=0, tiled=True)]
    dot_general x6 -> x0, matrix products: 17.2 us -> none  [the longest x3 9.41 us: layer(): part = jnp.dot(states, theirs, preferred_element_type=jnp.float32)]
    gather x9 -> x2, local copies, waits for them, and re-layouts: 15.2 us -> 2.53 us  [rows_at(): return x.at[index].get(mode='promise_in_bounds')]
    all_to_all x3, waiting for transfers between devices: 16.3 us -> 6.4 us  [spread(): lax.all_to_all(jnp.broadcast_to(x[None], (dps, *x.shape)), 'dp', split_ax...]
    all_gather x1, blocking collectives: 5.42 us -> 13.9 us  [on_device(): lax.all_gather(jnp.concatenate(exits, axis=0), 'section', axis=0)]
  transfers between devices with their start and end apart: 31 -> 28, of which waited for: 10 -> 6; matrix products, arithmetic and copies ran while one was open for 18% -> 11% of each run, Pallas kernels for 0% -> 15%
where the time goes in v4:
time: 284 us; the launch traced here: 282 us
  starting transfers between devices  91 us (32%)
  blocking collectives  51.9 us (18%)
  waiting for transfers between devices  49.7 us (18%)
  Pallas kernels  48.2 us (17%)
  other arithmetic  17.7 us (6%)
  matrix products  11.6 us (4%)
  local copies, waits for them, and re-layouts  11 us (4%)
    ppermute x22, starting transfers between devices, send(): lax.ppermute(x, AXES, [(a * dps + i, b * dps + (i ^ flip)) for a, b, flip...  58.3 us
    ppermute x22, waiting for transfers between devices, send(): lax.ppermute(x, AXES, [(a * dps + i, b * dps + (i ^ flip)) for a, b, flip...  31.5 us
    all_gather x1, blocking collectives, on_device(): owner_queries = lax.all_gather(queries, 'section', axis=0, tiled=True)  26.1 us
    pallas_call x3, Pallas kernels, kept_half(): pl.pallas_call(functools.partial(kept_kernel, width), out_shape=jax.Shape...  20 us
    pallas_call x3, Pallas kernels, sent_half(): pl.pallas_call(sent_kernel, out_shape=(jax.ShapeDtypeStruct((tokens, cols...  18.4 us
    all_gather x1, blocking collectives, on_device(): lax.all_gather(jnp.concatenate(exits, axis=0), 'section', axis=0)  13.9 us
    all_to_all x3, starting transfers between devices, spread(): lax.all_to_all(jnp.broadcast_to(x[None], (dps, *x.shape)), 'dp', split_ax...  13.5 us
    all_to_all x1, waiting for transfers between devices, on_device(): lax.all_to_all(received_grad, 'dp', split_axis=0, concat_axis=0, tiled=True)  11.8 us
  transfers between devices with their start and end apart: 28, of which 6 were waited for; matrix products, arithmetic and copies ran while one was open for 11% of the time, Pallas kernels for 15%

profile of v4, /device:TPU:0, one launch (start us, length us, event | category | flops | bytes accessed | tf_op | source)
XLA Modules:
  0.0 282.4 jit_solution(10039159933395505659)
XLA Ops:
  3.0 4.9 %collective-permute-start = (bf16[64,2048]{1,0:T(8,128)(2,1)}, bf16[64,2048]{1,0:T(8,128)(2,1)}, u32[]{:S(2)}, u32[]{:S(2)}) collective-permute-start(bf16[64,2048]{1,0:T(8,128)(2,1)} %get-tuple-element.20), channel_id=1, source_target_pairs={{0,1},{1,0},{2,3},{3,2},{4,5},{5,4},{6,7},{7,6},{16,17},{17,16},{1... | collective-permute-start | bytes 786440 | tf_op jit(solution)/shard_map/ppermute | solution.py:181
  10.8 4.9 %all-to-all-start.1 = ((bf16[8,8,4736]{2,1,0:T(8,128)(2,1)}), bf16[8,8,4736]{2,1,0:T(8,128)(2,1)S(1)}, u32[]{:S(2)}, u32[]{:S(2)}) async-start(bf16[8,8,4736]{2,1,0:T(8,128)(2,1)} %pad_maximum_fusion.1), calls=%async_computation.1 | async-start | bytes 1212416 | tf_op jit(solution)/shard_map/all_to_all | solution.py:240
  16.2 5.0 %shard_map.130 = bf16[2048,512]{1,0:T(8,128)(2,1)} custom-call(s32[4]{0:T(128)} %add_subtract_fusion.at_ref, bf16[4096,512]{1,0:T(8,128)(2,1)} %bitcast.82, f32[8,1,512]{2,1,0:T(1,128)} %bitcast.91), custom_call_target="tpu_custom_call" | custom-call | flops 1048576 | bytes 4194304 | tf_op jit(solution)/shard_map/pallas_call | solution.py:33
  21.2 3.9 %collective-permute-start.4 = (bf16[2048,512]{1,0:T(8,128)(2,1)}, bf16[2048,512]{1,0:T(8,128)(2,1)S(1)}, u32[]{:S(2)}, u32[]{:S(2)}) collective-permute-start(bf16[2048,512]{1,0:T(8,128)(2,1)} %shard_map.130), channel_id=1, source_target_pairs={{0,1},{1,0},{2,3},{3,2},{4,5},{5,4},{6,7},{7,6}} | collective-permute-start | bytes 6291464 | tf_op jit(solution)/shard_map/ppermute | solution.py:181
  27.1 5.2 %collective-permute-start.3 = (bf16[128,2048]{1,0:T(8,128)(2,1)}, bf16[128,2048]{1,0:T(8,128)(2,1)}, u32[]{:S(2)}, u32[]{:S(2)}) collective-permute-start(bf16[128,2048]{1,0:T(8,128)(2,1)} %maximum_select_fusion), channel_id=1, source_target_pairs={{0,6},{1,7},{2,4},{3,5},{4,2},{5,3},{6,0},{7,1},{16,22},{17,23},{1... | collective-permute-start | bytes 1572872 | tf_op jit(solution)/shard_map/ppermute | solution.py:181
  41.9 14.3 %collective-permute-done.2 = bf16[128,2048]{1,0:T(8,128)(2,1)} collective-permute-done((bf16[128,2048]{1,0:T(8,128)(2,1)}, bf16[128,2048]{1,0:T(8,128)(2,1)}, u32[]{:S(2)}, u32[]{:S(2)}) %collective-permute-start.2) | collective-permute-done | bytes 524320 | tf_op jit(solution)/shard_map/ppermute | solution.py:181
  65.1 4.9 %shard_map.129.refs_1_.refs_5_ = bf16[2048,512]{1,0:T(8,128)(2,1)} custom-call(s32[4]{0:T(128)} %fusion.25.at_ref, bf16[4096,512]{1,0:T(8,128)(2,1)} %bitcast.83, f32[8,1,512]{2,1,0:T(1,128)} %bitcast.92), custom_call_target="tpu_custom_call" | custom-call | flops 1048576 | bytes 4194304 | tf_op jit(solution)/shard_map/pallas_call | solution.py:33
  75.6 5.7 %shard_map.131 = (bf16[512,640]{1,0:T(8,128)(2,1)}, f32[512,128]{1,0:T(8,128)}) custom-call(s32[3]{0:T(128)} %pad_add_fusion.1.where_ref, bf16[512,2048]{1,0:T(8,128)(2,1)} %pad_maximum_fusion.refs_0_.refs_4_, bf16[2048,512]{1,0:T(8,128)(2,1)} %copy-done.2), custom_call_target="tpu_custom_call" | custom-call | flops 1073741824 | bytes 4194304 | tf_op jit(solution)/shard_map/pallas_call | solution.py:106
  85.3 26.1 %all_gather.15 = bf16[32,4096]{1,0:T(8,128)(2,1)} all-gather(bf16[8,4096]{1,0:T(8,128)(2,1)S(1)} %copy-done.7), channel_id=1, replica_groups=mesh['section'=4,'dp'=8] {'section'}, dimensions={0}, use_global_device_ids=true | all-gather | bytes 327680 | tf_op jit(solution)/shard_map/all_gather | solution.py:241
  112.6 6.3 %shard_map.132 = bf16[512,512]{1,0:T(8,128)(2,1)} custom-call(s32[3]{0:T(128)} %pad_add_fusion.1.where_ref, bf16[512,2048]{1,0:T(8,128)(2,1)} %pad_maximum_fusion.refs_0_.refs_4_, bf16[2048,512]{1,0:T(8,128)(2,1)} %shard_map.129.refs_1_.refs_5_, bf16[512,640]{1,0:T(8,128)(2,1)} %copy-done.6, f32[512,128]{1,0:T(8,128)} %get-tuple-element.12.refs_3_, ...), custom_call_target="tpu_custom_call" | custom-call | flops 1073741824 | bytes 4194304 | tf_op jit(solution)/shard_map/pallas_call | solution.py:133
  118.9 6.1 %collective-permute-start.9 = (bf16[512,512]{1,0:T(8,128)(2,1)}, bf16[512,512]{1,0:T(8,128)(2,1)}, u32[]{:S(2)}, u32[]{:S(2)}) collective-permute-start(bf16[512,512]{1,0:T(8,128)(2,1)} %shard_map.132), channel_id=1, source_target_pairs={{0,14},{1,15},{2,12},{3,13},{4,10},{5,11},{6,8},{7,9}} | collective-permute-start | bytes 1572872 | tf_op jit(solution)/shard_map/ppermute | solution.py:181
  136.9 5.6 %collective-permute-done.7.refs_1_ = bf16[512,512]{1,0:T(8,128)(2,1)} collective-permute-done((bf16[512,512]{1,0:T(8,128)(2,1)}, bf16[512,512]{1,0:T(8,128)(2,1)}, u32[]{:S(2)}, u32[]{:S(2)}) %collective-permute-start.7) | collective-permute-done | bytes 524320 | tf_op jit(solution)/shard_map/ppermute | solution.py:181
  142.5 6.3 %shard_map.133 = (bf16[512,640]{1,0:T(8,128)(2,1)}, f32[512,128]{1,0:T(8,128)}) custom-call(s32[3]{0:T(128)} %pad_add_fusion.where_ref, bf16[512,512]{1,0:T(8,128)(2,1)} %collective-permute-done.6.refs_0_, bf16[512,512]{1,0:T(8,128)(2,1)} %collective-permute-done.7.refs_1_, bf16[512,512]{1,0:T(8,128)(2,1)} %collective-permute-done.8.refs_2_, ...), custom_call_target="tpu_custom_call" | custom-call | flops 1073741824 | bytes 4194304 | tf_op jit(solution)/shard_map/pallas_call | solution.py:106
  156.7 6.5 %all-to-all-start.3 = ((bf16[8,4,512]{2,1,0:T(4,128)(2,1)}), bf16[8,4,512]{2,1,0:T(4,128)(2,1)S(1)}, u32[]{:S(2)}, u32[]{:S(2)}) async-start(bf16[8,4,512]{2,1,0:T(4,128)(2,1)} %broadcast_in_dim.64), calls=%async_computation.3 | async-start | bytes 65536 | tf_op jit(solution)/shard_map/all_to_all | solution.py:285
  163.5 6.4 %all-to-all-done.3 = bf16[8,4,512]{2,1,0:T(4,128)(2,1)S(1)} async-done(((bf16[8,4,512]{2,1,0:T(4,128)(2,1)}), bf16[8,4,512]{2,1,0:T(4,128)(2,1)S(1)}, u32[]{:S(2)}, u32[]{:S(2)}) %all-to-all-start.3) | async-done | bytes 32800 | tf_op jit(solution)/shard_map/all_to_all | solution.py:285
  170.0 6.8 %shard_map.134 = bf16[512,512]{1,0:T(8,128)(2,1)} custom-call(s32[3]{0:T(128)} %pad_add_fusion.where_ref, bf16[512,512]{1,0:T(8,128)(2,1)} %collective-permute-done.6.refs_0_, bf16[512,512]{1,0:T(8,128)(2,1)} %collective-permute-done.7.refs_1_, bf16[512,512]{1,0:T(8,128)(2,1)} %collective-permute-done.8.refs_2_, ...), custom_call_target="tpu_custom_call" | custom-call | flops 1073741824 | bytes 4194304 | tf_op jit(solution)/shard_map/pallas_call | solution.py:133
  187.8 13.9 %all-gather.1 = bf16[4,12,512]{2,1,0:T(8,128)(2,1)S(1)} all-gather(bf16[1,12,512]{2,1,0:T(8,128)(2,1)S(1)} %maximum_bitcast_fusion), channel_id=2, replica_groups=mesh['section'=4,'dp'=8] {'section'}, dimensions={0}, use_global_device_ids=true | all-gather | bytes 61440 | tf_op jit(solution)/shard_map/all_gather | solution.py:308
  207.2 6.4 %shard_map.135 = (bf16[512,640]{1,0:T(8,128)(2,1)}, f32[512,128]{1,0:T(8,128)}) custom-call(s32[3]{0:T(128)} %pad_add_fusion.where_ref, bf16[512,512]{1,0:T(8,128)(2,1)} %collective-permute-done.13.refs_0_, bf16[512,512]{1,0:T(8,128)(2,1)} %collective-permute-done.14.refs_1_, bf16[512,512]{1,0:T(8,128)(2,1)} %collective-permute-done.15.refs_2_, ...), custom_call_target="tpu_custom_call" | custom-call | flops 1073741824 | bytes 4194304 | tf_op jit(solution)/shard_map/pallas_call | solution.py:106
  218.3 8.7 %collective-permute-done.18.refs_6_ = bf16[512,640]{1,0:T(8,128)(2,1)S(1)} collective-permute-done((bf16[512,640]{1,0:T(8,128)(2,1)}, bf16[512,640]{1,0:T(8,128)(2,1)S(1)}, u32[]{:S(2)}, u32[]{:S(2)}) %collective-permute-start.18) | collective-permute-done | bytes 655392 | tf_op jit(solution)/shard_map/ppermute | solution.py:181
  227.8 6.9 %shard_map.136 = bf16[512,512]{1,0:T(8,128)(2,1)} custom-call(s32[3]{0:T(128)} %pad_add_fusion.where_ref, bf16[512,512]{1,0:T(8,128)(2,1)} %collective-permute-done.13.refs_0_, bf16[512,512]{1,0:T(8,128)(2,1)} %collective-permute-done.14.refs_1_, bf16[512,512]{1,0:T(8,128)(2,1)} %collective-permute-done.15.refs_2_, ...), custom_call_target="tpu_custom_call" | custom-call | flops 1073741824 | bytes 4194304 | tf_op jit(solution)/shard_map/pallas_call | solution.py:133
  234.7 8.4 %all-to-all-start = ((bf16[8,64,512]{2,1,0:T(8,128)(2,1)}), bf16[8,64,512]{2,1,0:T(8,128)(2,1)S(1)}, u32[]{:S(2)}, u32[]{:S(2)}) async-start(bf16[8,64,512]{2,1,0:T(8,128)(2,1)} %bitcast.86), calls=%async_computation | async-start | bytes 1048576 | tf_op jit(solution)/shard_map/all_to_all | solution.py:280
  244.7 11.8 %all_gather.14 = f32[32,64]{1,0:T(8,128)S(1)} all-gather(f32[8,64]{1,0:T(8,128)S(1)} %select_reduce_fusion), channel_id=1, replica_groups=mesh['section'=4,'dp'=8] {'section'}, dimensions={0}, use_global_device_ids=true | all-gather | bytes 10240 | tf_op jit(solution)/shard_map/all_gather | solution.py:339
  257.9 5.9 %all-to-all-start.5 = ((bf16[8,8,4096]{2,1,0:T(8,128)(2,1)}), bf16[8,8,4096]{2,1,0:T(8,128)(2,1)S(1)}, u32[]{:S(2)}, u32[]{:S(2)}) async-start(bf16[8,8,4096]{2,1,0:T(8,128)(2,1)} %fusion.1), calls=%async_computation.5 | async-start | bytes 1048576 | tf_op jit(solution)/shard_map/all_to_all | solution.py:344
  267.1 11.8 %all-to-all-done.5 = bf16[8,8,4096]{2,1,0:T(8,128)(2,1)S(1)} async-done(((bf16[8,8,4096]{2,1,0:T(8,128)(2,1)}), bf16[8,8,4096]{2,1,0:T(8,128)(2,1)S(1)}, u32[]{:S(2)}, u32[]{:S(2)}) %all-to-all-start.5) | async-done | bytes 524320 | tf_op jit(solution)/shard_map/all_to_all | solution.py:344
  (145 shorter events, 88.5 us)
Async XLA Ops:
  3.0 22.1 %collective-permute-start = (bf16[64,2048]{1,0:T(8,128)(2,1)}, bf16[64,2048]{1,0:T(8,128)(2,1)}, u32[]{:S(2)}, u32[]{:S(2)}) collective-permute-start(bf16[64,2048]{1,0:T(8,128)(2,1)} %get-tuple-element.20), channel_id=1, source_target_pairs={{0,1},{1,0},{2,3},{3,2},{4,5},{5,4},{6,7},{7,6},{16,17},{17,16},{1... | collective-permute-start | bytes 786440 | tf_op jit(solution)/shard_map/ppermute | solution.py:181
  10.8 49.8 %all-to-all-start.1 = ((bf16[8,8,4736]{2,1,0:T(8,128)(2,1)}), bf16[8,8,4736]{2,1,0:T(8,128)(2,1)S(1)}, u32[]{:S(2)}, u32[]{:S(2)}) async-start(bf16[8,8,4736]{2,1,0:T(8,128)(2,1)} %pad_maximum_fusion.1), calls=%async_computation.1 | async-start | bytes 1212416 | tf_op jit(solution)/shard_map/all_to_all | solution.py:240
  21.2 53.1 %collective-permute-start.4 = (bf16[2048,512]{1,0:T(8,128)(2,1)}, bf16[2048,512]{1,0:T(8,128)(2,1)S(1)}, u32[]{:S(2)}, u32[]{:S(2)}) collective-permute-start(bf16[2048,512]{1,0:T(8,128)(2,1)} %shard_map.130), channel_id=1, source_target_pairs={{0,1},{1,0},{2,3},{3,2},{4,5},{5,4},{6,7},{7,6}} | collective-permute-start | bytes 6291464 | tf_op jit(solution)/shard_map/ppermute | solution.py:181
  27.1 14.8 %collective-permute-start.3 = (bf16[128,2048]{1,0:T(8,128)(2,1)}, bf16[128,2048]{1,0:T(8,128)(2,1)}, u32[]{:S(2)}, u32[]{:S(2)}) collective-permute-start(bf16[128,2048]{1,0:T(8,128)(2,1)} %maximum_select_fusion), channel_id=1, source_target_pairs={{0,6},{1,7},{2,4},{3,5},{4,2},{5,3},{6,0},{7,1},{16,22},{17,23},{1... | collective-permute-start | bytes 1572872 | tf_op jit(solution)/shard_map/ppermute | solution.py:181
  32.3 24.0 %collective-permute-start.2 = (bf16[128,2048]{1,0:T(8,128)(2,1)}, bf16[128,2048]{1,0:T(8,128)(2,1)}, u32[]{:S(2)}, u32[]{:S(2)}) collective-permute-start(bf16[128,2048]{1,0:T(8,128)(2,1)} %maximum_select_fusion), channel_id=1, source_target_pairs={{0,4},{1,5},{2,6},{3,7},{4,0},{5,1},{6,2},{7,3},{16,20},{17,21},{1... | collective-permute-start | bytes 1572872 | tf_op jit(solution)/shard_map/ppermute | solution.py:181
  34.2 22.0 %collective-permute-start.1 = (bf16[128,2048]{1,0:T(8,128)(2,1)}, bf16[128,2048]{1,0:T(8,128)(2,1)}, u32[]{:S(2)}, u32[]{:S(2)}) collective-permute-start(bf16[128,2048]{1,0:T(8,128)(2,1)} %maximum_select_fusion), channel_id=1, source_target_pairs={{0,2},{1,3},{2,0},{3,1},{4,6},{5,7},{6,4},{7,5},{16,18},{17,19},{1... | collective-permute-start | bytes 1572872 | tf_op jit(solution)/shard_map/ppermute | solution.py:181
  37.2 92.0 %collective-permute-start.11 = (bf16[2048,512]{1,0:T(8,128)(2,1)}, bf16[2048,512]{1,0:T(8,128)(2,1)}, u32[]{:S(2)}, u32[]{:S(2)}) collective-permute-start(bf16[2048,512]{1,0:T(8,128)(2,1)} %shard_map.130), channel_id=1, source_target_pairs={{8,9},{9,8},{10,11},{11,10},{12,13},{13,12},{14,15},{15,14},{16,17... | collective-permute-start | bytes 6291464 | tf_op jit(solution)/shard_map/ppermute | solution.py:181
  59.3 73.5 %collective-permute-start.10 = (bf16[512,2048]{1,0:T(8,128)(2,1)}, bf16[512,2048]{1,0:T(8,128)(2,1)}, u32[]{:S(2)}, u32[]{:S(2)}) collective-permute-start(bf16[512,2048]{1,0:T(8,128)(2,1)} %pad_maximum_fusion.refs_0_.refs_4_), channel_id=1, source_target_pairs={{16,0},{17,1},{18,2},{19,3},{20,4},{21,5},{22,6},{23,7}} | collective-permute-start | bytes 6291464 | tf_op jit(solution)/shard_map/ppermute | solution.py:181
  70.6 40.8 %all-to-all-start.2 = ((bf16[8,4,512]{2,1,0:T(4,128)(2,1)}), bf16[8,4,512]{2,1,0:T(4,128)(2,1)S(1)}, u32[]{:S(2)}, u32[]{:S(2)}) async-start(bf16[8,4,512]{2,1,0:T(4,128)(2,1)} %broadcast_in_dim.63), calls=%async_computation.2 | async-start | bytes 65536 | tf_op jit(solution)/shard_map/all_to_all | solution.py:285
  81.4 30.3 %collective-permute-start.5 = (bf16[512,640]{1,0:T(8,128)(2,1)}, bf16[512,640]{1,0:T(8,128)(2,1)S(1)}, u32[]{:S(2)}, u32[]{:S(2)}) collective-permute-start(bf16[512,640]{1,0:T(8,128)(2,1)} %get-tuple-element.11), channel_id=1, source_target_pairs={{0,1},{1,0},{2,3},{3,2},{4,5},{5,4},{6,7},{7,6}} | collective-permute-start | bytes 1966088 | tf_op jit(solution)/shard_map/ppermute | solution.py:181
  118.9 15.2 %collective-permute-start.9 = (bf16[512,512]{1,0:T(8,128)(2,1)}, bf16[512,512]{1,0:T(8,128)(2,1)}, u32[]{:S(2)}, u32[]{:S(2)}) collective-permute-start(bf16[512,512]{1,0:T(8,128)(2,1)} %shard_map.132), channel_id=1, source_target_pairs={{0,14},{1,15},{2,12},{3,13},{4,10},{5,11},{6,8},{7,9}} | collective-permute-start | bytes 1572872 | tf_op jit(solution)/shard_map/ppermute | solution.py:181
  127.1 15.4 %collective-permute-start.7 = (bf16[512,512]{1,0:T(8,128)(2,1)}, bf16[512,512]{1,0:T(8,128)(2,1)}, u32[]{:S(2)}, u32[]{:S(2)}) collective-permute-start(bf16[512,512]{1,0:T(8,128)(2,1)} %shard_map.132), channel_id=1, source_target_pairs={{0,10},{1,11},{2,8},{3,9},{4,14},{5,15},{6,12},{7,13}} | collective-permute-start | bytes 1572872 | tf_op jit(solution)/shard_map/ppermute | solution.py:181
  129.2 13.3 %collective-permute-start.6 = (bf16[512,512]{1,0:T(8,128)(2,1)}, bf16[512,512]{1,0:T(8,128)(2,1)}, u32[]{:S(2)}, u32[]{:S(2)}) collective-permute-start(bf16[512,512]{1,0:T(8,128)(2,1)} %shard_map.132), channel_id=1, source_target_pairs={{0,8},{1,9},{2,10},{3,11},{4,12},{5,13},{6,14},{7,15}} | collective-permute-start | bytes 1572872 | tf_op jit(solution)/shard_map/ppermute | solution.py:181
  132.8 73.1 %collective-permute-start.17 = (bf16[512,2048]{1,0:T(8,128)(2,1)}, bf16[512,2048]{1,0:T(8,128)(2,1)S(1)}, u32[]{:S(2)}, u32[]{:S(2)}) collective-permute-start(bf16[512,2048]{1,0:T(8,128)(2,1)} %pad_maximum_fusion.refs_0_.refs_4_), channel_id=1, source_target_pairs={{24,0},{25,1},{26,2},{27,3},{28,4},{29,5},{30,6},{31,7}} | collective-permute-start | bytes 6291464 | tf_op jit(solution)/shard_map/ppermute | solution.py:181
  148.8 21.2 %collective-permute-start.12 = (bf16[512,640]{1,0:T(8,128)(2,1)}, bf16[512,640]{1,0:T(8,128)(2,1)}, u32[]{:S(2)}, u32[]{:S(2)}) collective-permute-start(bf16[512,640]{1,0:T(8,128)(2,1)} %get-tuple-element.13), channel_id=1, source_target_pairs={{0,1},{1,0},{2,3},{3,2},{4,5},{5,4},{6,7},{7,6},{8,9},{9,8},{10,11... | collective-permute-start | bytes 1966088 | tf_op jit(solution)/shard_map/ppermute | solution.py:181
  156.7 13.2 %all-to-all-start.3 = ((bf16[8,4,512]{2,1,0:T(4,128)(2,1)}), bf16[8,4,512]{2,1,0:T(4,128)(2,1)S(1)}, u32[]{:S(2)}, u32[]{:S(2)}) async-start(bf16[8,4,512]{2,1,0:T(4,128)(2,1)} %broadcast_in_dim.64), calls=%async_computation.3 | async-start | bytes 65536 | tf_op jit(solution)/shard_map/all_to_all | solution.py:285
  183.4 22.5 %collective-permute-start.16 = (bf16[512,512]{1,0:T(8,128)(2,1)}, bf16[512,512]{1,0:T(8,128)(2,1)}, u32[]{:S(2)}, u32[]{:S(2)}) collective-permute-start(bf16[512,512]{1,0:T(8,128)(2,1)} %collective-permute-done.13.refs_0_), channel_id=1, source_target_pairs={{8,14},{9,15},{10,12},{11,13},{12,10},{13,11},{14,8},{15,9},{16,22... | collective-permute-start | bytes 1572872 | tf_op jit(solution)/shard_map/ppermute | solution.py:181
  184.9 21.0 %collective-permute-start.15 = (bf16[512,512]{1,0:T(8,128)(2,1)}, bf16[512,512]{1,0:T(8,128)(2,1)}, u32[]{:S(2)}, u32[]{:S(2)}) collective-permute-start(bf16[512,512]{1,0:T(8,128)(2,1)} %collective-permute-done.13.refs_0_), channel_id=1, source_target_pairs={{8,12},{9,13},{10,14},{11,15},{12,8},{13,9},{14,10},{15,11},{16,20... | collective-permute-start | bytes 1572872 | tf_op jit(solution)/shard_map/ppermute | solution.py:181
  186.4 19.5 %collective-permute-start.14 = (bf16[512,512]{1,0:T(8,128)(2,1)}, bf16[512,512]{1,0:T(8,128)(2,1)}, u32[]{:S(2)}, u32[]{:S(2)}) collective-permute-start(bf16[512,512]{1,0:T(8,128)(2,1)} %collective-permute-done.13.refs_0_), channel_id=1, source_target_pairs={{8,10},{9,11},{10,8},{11,9},{12,14},{13,15},{14,12},{15,13},{16,18... | collective-permute-start | bytes 1572872 | tf_op jit(solution)/shard_map/ppermute | solution.py:181
  202.5 14.9 %all-to-all-start.4 = ((bf16[8,12,512]{2,1,0:T(8,128)(2,1)}), bf16[8,12,512]{2,1,0:T(8,128)(2,1)S(1)}, u32[]{:S(2)}, u32[]{:S(2)}) async-start(bf16[8,12,512]{2,1,0:T(8,128)(2,1)} %broadcast_in_dim.104), calls=%async_computation.4 | async-start | bytes 262144 | tf_op jit(solution)/shard_map/all_to_all | solution.py:285
  213.6 13.4 %collective-permute-start.18 = (bf16[512,640]{1,0:T(8,128)(2,1)}, bf16[512,640]{1,0:T(8,128)(2,1)S(1)}, u32[]{:S(2)}, u32[]{:S(2)}) collective-permute-start(bf16[512,640]{1,0:T(8,128)(2,1)} %get-tuple-element.15), channel_id=1, source_target_pairs={{0,1},{1,0},{2,3},{3,2},{4,5},{5,4},{6,7},{7,6},{8,9},{9,8},{10,11... | collective-permute-start | bytes 1966088 | tf_op jit(solution)/shard_map/ppermute | solution.py:181
  234.7 23.2 %all-to-all-start = ((bf16[8,64,512]{2,1,0:T(8,128)(2,1)}), bf16[8,64,512]{2,1,0:T(8,128)(2,1)S(1)}, u32[]{:S(2)}, u32[]{:S(2)}) async-start(bf16[8,64,512]{2,1,0:T(8,128)(2,1)} %bitcast.86), calls=%async_computation | async-start | bytes 1048576 | tf_op jit(solution)/shard_map/all_to_all | solution.py:280
  257.9 20.9 %all-to-all-start.5 = ((bf16[8,8,4096]{2,1,0:T(8,128)(2,1)}), bf16[8,8,4096]{2,1,0:T(8,128)(2,1)S(1)}, u32[]{:S(2)}, u32[]{:S(2)}) async-start(bf16[8,8,4096]{2,1,0:T(8,128)(2,1)} %fusion.1), calls=%async_computation.5 | async-start | bytes 1048576 | tf_op jit(solution)/shard_map/all_to_all | solution.py:344
  264.0 16.5 %collective-permute-start.19 = (bf16[64,4096]{1,0:T(8,128)(2,1)S(1)}, bf16[64,4096]{1,0:T(8,128)(2,1)S(1)}, u32[]{:S(2)}, u32[]{:S(2)}) collective-permute-start(bf16[64,4096]{1,0:T(8,128)(2,1)S(1)} %bitcast.90), channel_id=1, source_target_pairs={{0,8},{1,9},{2,10},{3,11},{4,12},{5,13},{6,14},{7,15},{8,16},{9,17... | collective-permute-start | bytes 1572872 | tf_op jit(solution)/shard_map/ppermute | solution.py:181
  (17 other events, 171.5 us)
